TPU v7x, 128 devices: a whole 4x4x4 slice. The times are simulated.
128 devices in a mesh: ctx: 16 (over y_hi, x, core), wa: 8 (over y_lo, z).
Axes of the slice: x: 4, y: 4 (y_hi: 2, y_lo: 2; y = y_hi * 2 + y_lo), z: 4, core: 2. Of those that a mesh axis runs over, the one named last changes fastest.
Arguments:
- layer_input: bfloat16 [2048, 1024], P('ctx'), may hold values from -6 to 6
- block_order: int32 [32], replicated, may hold values from 0 to 31, each once
- seg_ids: int32 [2048], replicated, may hold values from 0 to 2, never falling along the last dimension, each value on 1 to 1024 neighbouring positions
- cotangent: bfloat16 [2048, 1024], P('ctx'), may hold values from -6 to 6
- ln1_gain: bfloat16 [1024], replicated, may hold values from 0.5 to 1.5
- ln1_bias: bfloat16 [1024], replicated, may hold values from -1.75 to 1.75
- w_qkv: bfloat16 [1024, 3, 1024], P(None, None, 'wa'), may hold values from -0.1875 to 0.1875
- b_qv: bfloat16 [2, 1024], P(None, 'wa'), may hold values from -1.75 to 1.75
- w_out: bfloat16 [1024, 1024], P('wa'), may hold values from -1.5 to 1.5
- b_out: bfloat16 [1024], replicated, may hold values from -1.75 to 1.75
- ln2_gain: bfloat16 [1024], replicated, may hold values from 0.5 to 1.5
- ln2_bias: bfloat16 [1024], replicated, may hold values from -1.75 to 1.75
- w_up: bfloat16 [1024, 4096], P(None, 'wa'), may hold values from -0.1875 to 0.1875
- b_up: bfloat16 [4096], P('wa'), may hold values from -1.75 to 1.75
- w_down: bfloat16 [4096, 1024], P('wa'), may hold values from -0.09375 to 0.09375
- b_down: bfloat16 [1024], replicated, may hold values from -1.75 to 1.75
Outputs:
- layer_output: bfloat16 [2048, 1024], P('ctx')
- grad_input: float32 [2048, 1024], P('ctx')
- grad_ln1_gain: float32 [1024], replicated
- grad_ln1_bias: float32 [1024], replicated
- grad_w_qkv: float32 [1024, 3, 1024], P(None, None, 'wa')
- grad_b_qv: float32 [2, 1024], P(None, 'wa')
- grad_w_out: float32 [1024, 1024], P('wa')
- grad_b_out: float32 [1024], replicated
- grad_ln2_gain: float32 [1024], replicated
- grad_ln2_bias: float32 [1024], replicated
- grad_w_up: float32 [1024, 4096], P(None, 'wa')
- grad_b_up: float32 [4096], P('wa')
- grad_w_down: float32 [4096, 1024], P('wa')
- grad_b_down: float32 [1024], replicated
Inputs may be any that keep to these rules, and one draw needn't show every extreme that they name: Each of the 32 stream blocks appears once; row block b of layer_input holds stream block block_order[b]. `seg_ids`: non-decreasing along the stream; each of the 3 sequences has 1 to 1024 positions, one exactly 1024.
All inputs are finite; a program needn't handle non-finite values.
Results may differ from a plain program's by a relative error of at most 0.02.
Values may be sent and summed in bfloat16 or wider, within the bound.
A program may use at most 64 MiB of HBM per device.

v0:
```python
import functools
import math

import jax
import jax.numpy as jnp
from jax import lax
from jax.sharding import PartitionSpec as P

HD = 64


def layer_norm(rows_in, gain_vec, offset):
    row_mean = jnp.mean(rows_in, -1, keepdims=True)
    centered = rows_in - row_mean
    variance = jnp.mean(centered * centered, -1, keepdims=True)
    return centered * lax.rsqrt(variance + 1e-05) * gain_vec + offset


def attend_back(
    query_heads,
    grad_heads,
    log_total,
    delta_rows,
    query_pos,
    query_seg,
    key_heads,
    value_heads,
    key_pos,
    key_seg,
):
    score_scale = HD ** (-0.5)
    allowed = (key_seg[None, :] == query_seg[:, None]) & (key_pos[None, :] <= query_pos[:, None])
    scores = (
        jnp.einsum("qhd,khd->hqk", query_heads, key_heads, preferred_element_type=jnp.float32)
        * score_scale
    )
    weights = jnp.where(
        allowed[None], jnp.exp(jnp.where(allowed[None], scores, -1e30) - log_total[:, :, None]), 0.0
    )
    grad_weights = jnp.einsum(
        "qhd,khd->hqk", grad_heads, value_heads, preferred_element_type=jnp.float32
    )
    grad_scores = (weights * (grad_weights - delta_rows[:, :, None])).astype(jnp.bfloat16)
    grad_query = (
        jnp.einsum("hqk,khd->qhd", grad_scores, key_heads, preferred_element_type=jnp.float32)
        * score_scale
    )
    grad_key = (
        jnp.einsum("hqk,qhd->khd", grad_scores, query_heads, preferred_element_type=jnp.float32)
        * score_scale
    )
    grad_value = jnp.einsum(
        "hqk,qhd->khd", weights, grad_heads.astype(jnp.float32), precision=lax.Precision.HIGHEST
    )
    return (grad_query, grad_key, grad_value)


def body(
    layer_input,
    block_order,
    seg_ids,
    cotangent,
    ln1_gain,
    ln1_bias,
    w_qkv,
    b_qv,
    w_out,
    b_out,
    ln2_gain,
    ln2_bias,
    w_up,
    b_up,
    w_down,
    b_down,
):
    local_rows = layer_input.shape[0]
    block_rows = local_rows // 2
    model_width = layer_input.shape[1]
    head_width = w_qkv.shape[2]
    head_count = head_width // HD
    score_scale = HD ** (-0.5)
    my_index = lax.axis_index("ctx")

    def row_total(left, right, pattern):
        return lax.psum(jnp.einsum(pattern, left, right, preferred_element_type=jnp.float32), "wa")

    def block_positions(first_row, row_count):
        row_index = first_row + jnp.arange(row_count, dtype=jnp.int32)
        return block_order[row_index // block_rows] * block_rows + row_index % block_rows

    my_pos = block_positions(my_index * local_rows, local_rows)
    my_seg = seg_ids[my_pos]
    x_float = layer_input.astype(jnp.float32)
    gain_one = ln1_gain.astype(jnp.float32)
    bias_one = ln1_bias.astype(jnp.float32)
    gain_two = ln2_gain.astype(jnp.float32)
    bias_two = ln2_bias.astype(jnp.float32)
    normed = layer_norm(x_float, gain_one, bias_one).astype(jnp.bfloat16)
    flat_qkv = w_qkv.reshape(model_width, 3 * head_width)
    projected = jnp.dot(normed, flat_qkv, preferred_element_type=jnp.float32).reshape(
        local_rows, 3, head_width
    )
    queries = (projected[:, 0] + b_qv[0].astype(jnp.float32)).astype(jnp.bfloat16)
    keys_local = projected[:, 1].astype(jnp.bfloat16)
    values_local = (projected[:, 2] + b_qv[1].astype(jnp.float32)).astype(jnp.bfloat16)
    query_heads = queries.reshape(local_rows, head_count, HD)
    run_max = jnp.full((head_count, local_rows), -1e30, jnp.float32)
    weighted = jnp.zeros((local_rows, head_count, HD), jnp.float32)
    key_piece = lax.all_gather(keys_local, "ctx", axis=0, tiled=True)
    value_piece = lax.all_gather(values_local, "ctx", axis=0, tiled=True)
    row_count = key_piece.shape[0]
    key_pos = block_positions(jnp.int32(0), row_count)
    key_seg = seg_ids[key_pos]
    allowed = (key_seg[None, :] == my_seg[:, None]) & (key_pos[None, :] <= my_pos[:, None])
    scores = (
        jnp.einsum(
            "qhd,khd->hqk",
            query_heads,
            key_piece.reshape(row_count, head_count, HD),
            preferred_element_type=jnp.float32,
        )
        * score_scale
    )
    masked = jnp.where(allowed[None], scores, -1e30)
    new_max = jnp.maximum(run_max, jnp.max(masked, -1))
    weights = jnp.where(allowed[None], jnp.exp(masked - new_max[:, :, None]), 0.0)
    factor = jnp.exp(run_max - new_max)
    run_sum = jnp.sum(weights, -1)
    mixed = jnp.einsum(
        "hqk,khd->qhd",
        weights,
        value_piece.reshape(row_count, head_count, HD).astype(jnp.float32),
        precision=lax.Precision.HIGHEST,
    )
    weighted = weighted * factor.T[:, :, None] + mixed
    run_max, run_sum, weighted = (new_max, run_sum, weighted)
    attn_raw = weighted / run_sum.T[:, :, None]
    log_total = run_max + jnp.log(run_sum)
    attn_low = attn_raw.reshape(local_rows, head_width).astype(jnp.bfloat16)
    attn_sum = row_total(attn_low, w_out, "tc,cd->td")
    hidden_res = x_float + attn_sum + b_out.astype(jnp.float32)
    normed_two = layer_norm(hidden_res, gain_two, bias_two).astype(jnp.bfloat16)
    up_proj = jnp.dot(normed_two, w_up, preferred_element_type=jnp.float32) + b_up.astype(
        jnp.float32
    )
    activated = jax.nn.gelu(up_proj, approximate=True).astype(jnp.bfloat16)
    mlp_sum = row_total(activated, w_down, "tf,fd->td")
    result = (hidden_res + mlp_sum + b_down.astype(jnp.float32)).astype(jnp.bfloat16)
    grad_out = cotangent.astype(jnp.float32)
    grad_w_down = jnp.einsum("tf,td->fd", activated, cotangent, preferred_element_type=jnp.float32)
    grad_b_down = jnp.sum(grad_out, 0)
    grad_act = jnp.einsum("td,fd->tf", cotangent, w_down, preferred_element_type=jnp.float32)
    gelu_value, gelu_back = jax.vjp(functools.partial(jax.nn.gelu, approximate=True), up_proj)
    grad_up = gelu_back(grad_act)[0].astype(jnp.bfloat16)
    grad_w_up = jnp.einsum("td,tf->df", normed_two, grad_up, preferred_element_type=jnp.float32)
    grad_b_up = jnp.sum(grad_up.astype(jnp.float32), 0)
    grad_normed_two = row_total(grad_up, w_up, "tf,df->td")
    norm_value, norm_back = jax.vjp(layer_norm, hidden_res, gain_two, bias_two)
    grad_res_ln, grad_ln2_gain, grad_ln2_bias = norm_back(grad_normed_two)
    grad_hidden = grad_out + grad_res_ln
    grad_hidden_low = grad_hidden.astype(jnp.bfloat16)
    grad_w_out = jnp.einsum(
        "tc,td->cd", attn_low, grad_hidden_low, preferred_element_type=jnp.float32
    )
    grad_b_out = jnp.sum(grad_hidden, 0)
    grad_attn = jnp.einsum(
        "td,cd->tc", grad_hidden_low, w_out, preferred_element_type=jnp.float32
    ).astype(jnp.bfloat16)
    grad_heads = grad_attn.reshape(local_rows, head_count, HD)
    delta_rows = jnp.sum(grad_heads.astype(jnp.float32) * attn_raw, -1).T
    whole_keys, whole_values = (
        lax.all_gather(keys_local, "ctx", axis=0, tiled=True),
        lax.all_gather(values_local, "ctx", axis=0, tiled=True),
    )
    all_rows = whole_keys.shape[0]
    key_rows = math.gcd(512, all_rows)
    key_blocks = all_rows // key_rows

    def key_step(grad_query_sum, block_index):
        first_row = block_index * key_rows
        key_block = lax.dynamic_slice_in_dim(whole_keys, first_row, key_rows, 0).reshape(
            key_rows, head_count, HD
        )
        value_block = lax.dynamic_slice_in_dim(whole_values, first_row, key_rows, 0).reshape(
            key_rows, head_count, HD
        )
        key_pos = block_positions(first_row, key_rows)
        grad_query, grad_key, grad_value = attend_back(
            query_heads,
            grad_heads,
            log_total,
            delta_rows,
            my_pos,
            my_seg,
            key_block,
            value_block,
            key_pos,
            seg_ids[key_pos],
        )
        return (
            grad_query_sum + grad_query,
            (grad_key.reshape(key_rows, head_width), grad_value.reshape(key_rows, head_width)),
        )

    grad_query_sum, key_terms = lax.scan(
        key_step,
        jnp.zeros((local_rows, head_count, HD), jnp.float32),
        jnp.arange(key_blocks, dtype=jnp.int32),
    )
    key_terms_all = key_terms[0].reshape(all_rows, head_width)
    value_terms_all = key_terms[1].reshape(all_rows, head_width)
    grad_key_mine, grad_value_mine = (
        lax.psum_scatter(key_terms_all, "ctx", scatter_dimension=0, tiled=True),
        lax.psum_scatter(value_terms_all, "ctx", scatter_dimension=0, tiled=True),
    )
    grad_query_low = grad_query_sum.reshape(local_rows, head_width).astype(jnp.bfloat16)
    grad_key_low = grad_key_mine.astype(jnp.bfloat16)
    grad_value_low = grad_value_mine.astype(jnp.bfloat16)
    grad_qkv = jnp.stack([grad_query_low, grad_key_low, grad_value_low], axis=1).reshape(
        local_rows, 3 * head_width
    )
    grad_w_qkv = jnp.einsum(
        "td,tc->dc", normed, grad_qkv, preferred_element_type=jnp.float32
    ).reshape(model_width, 3, head_width)
    grad_b_qv = jnp.stack(
        [
            jnp.sum(grad_query_low.astype(jnp.float32), 0),
            jnp.sum(grad_value_low.astype(jnp.float32), 0),
        ]
    )
    grad_normed = row_total(grad_qkv, flat_qkv, "tc,dc->td")
    first_value, first_back = jax.vjp(layer_norm, x_float, gain_one, bias_one)
    grad_x_ln, grad_ln1_gain, grad_ln1_bias = first_back(grad_normed)
    grad_input = grad_hidden + grad_x_ln
    summed = (
        lax.psum(grad_ln1_gain.astype(jnp.bfloat16), "ctx").astype(jnp.float32),
        lax.psum(grad_ln1_bias.astype(jnp.bfloat16), "ctx").astype(jnp.float32),
        lax.psum(grad_w_qkv.astype(jnp.bfloat16), "ctx").astype(jnp.float32),
        lax.psum(grad_b_qv.astype(jnp.bfloat16), "ctx").astype(jnp.float32),
        lax.psum(grad_w_out.astype(jnp.bfloat16), "ctx").astype(jnp.float32),
        lax.psum(grad_b_out.astype(jnp.bfloat16), "ctx").astype(jnp.float32),
        lax.psum(grad_ln2_gain.astype(jnp.bfloat16), "ctx").astype(jnp.float32),
        lax.psum(grad_ln2_bias.astype(jnp.bfloat16), "ctx").astype(jnp.float32),
        lax.psum(grad_w_up.astype(jnp.bfloat16), "ctx").astype(jnp.float32),
        lax.psum(grad_b_up.astype(jnp.bfloat16), "ctx").astype(jnp.float32),
        lax.psum(grad_w_down.astype(jnp.bfloat16), "ctx").astype(jnp.float32),
        lax.psum(grad_b_down.astype(jnp.bfloat16), "ctx").astype(jnp.float32),
    )
    return (
        result,
        grad_input,
        summed[0],
        summed[1],
        summed[2],
        summed[3],
        summed[4],
        summed[5],
        summed[6],
        summed[7],
        summed[8],
        summed[9],
        summed[10],
        summed[11],
    )


def solution(mesh):
    placed = (
        P("ctx", None),
        P(),
        P(),
        P("ctx", None),
        P(),
        P(),
        P(None, None, "wa"),
        P(None, "wa"),
        P("wa", None),
        P(),
        P(),
        P(),
        P(None, "wa"),
        P("wa"),
        P("wa", None),
        P(),
    )
    return jax.shard_map(
        body,
        mesh=mesh,
        in_specs=placed,
        out_specs=(
            P("ctx", None),
            P("ctx", None),
            P(),
            P(),
            P(None, None, "wa"),
            P(None, "wa"),
            P("wa", None),
            P(),
            P(),
            P(),
            P(None, "wa"),
            P("wa"),
            P("wa", None),
            P(),
        ),
        check_vma=False,
    )
```

profile of v0, /device:TPU:1, one launch (start us, length us, event | category | flops | bytes accessed | tf_op | source)
XLA Modules:
  0.0 775.0 jit_solution(5586728782206666742)
XLA Ops:
  16.9 28.5 %all-gather = bf16[2048,1,128]{0,2,1:T(8,128)(2,1)} all-gather(bf16[128,1,128]{0,2,1:T(8,128)(2,1)S(1)} %slice.138), channel_id=2, replica_groups=mesh['ctx'=16,'wa'=8] {'ctx'}, dimensions={0}, use_global_device_ids=true | all-gather | bytes 557056 | tf_op jit(solution)/shard_map/all_gather | solution.py:109
  45.4 4.5 compare_select_fusion.13
  49.9 15.8 %fusion.52 = (s32[2048]{0:T(1024)S(1)}, s32[2048]{0:T(1024)S(1)}) fusion(pred[2048]{0:T(1024)(128)(4,1)S(1)} %compare_reduce_fusion.25, pred[2048]{0:T(1024)(128)(4,1)S(1)} %compare_reduce_fusion.26, pred[2048]{0:T(1024)(128)(4,1)S(1)} %compare_reduce_fusion.27, pred[2048]{0:T(1024)(128)(4,1)S(1)} %compare_reduce_fusion.28, ...), kind=kLoop, calls=%fused_computation.179 | loop fusion | flops 67584 | bytes 75876 | tf_op jit(solution)/shard_map/add | solution.py:89
  65.8 11.8 %gather_fusion.1 = s32[2048]{0:T(1024)S(1)} fusion(s32[2048]{0:T(1024)S(1)} %copy-done.1, s32[2048]{0:T(1024)S(1)} %broadcast_clamp_fusion), kind=kCustom, calls=%fused_computation.1 | custom fusion | bytes 24576 | tf_op jit(solution)/shard_map/gather | solution.py:113
  79.1 1.7 fusion.78
  81.0 22.1 %all_gather.9 = bf16[2048,128]{0,1:T(8,128)(2,1)} all-gather(bf16[128,128]{0,1:T(8,128)(2,1)S(1)} %fusion.50), channel_id=1, replica_groups=mesh['ctx'=16,'wa'=8] {'ctx'}, dimensions={0}, use_global_device_ids=true | all-gather | bytes 557056 | tf_op jit(solution)/shard_map/all_gather | solution.py:110
  104.2 3.5 fusion.79
  109.4 67.9 %all-reduce.8.cloned.1.call-done = f32[128,1024]{1,0:T(8,128)} async-done(((f32[128,1024]{1,0:T(8,128)}), f32[128,1024]{1,0:T(8,128)}) %all-reduce.8.cloned.1.call-update) | async-done | bytes 524304 | tf_op jit(solution)/shard_map/psum | solution.py:85
  178.8 1.8 fusion.68
  182.0 74.5 %all-reduce.10.cloned.1.call-done = f32[128,1024]{1,0:T(8,128)} async-done(((f32[128,1024]{1,0:T(8,128)}), f32[128,1024]{1,0:T(8,128)}) %all-reduce.10.cloned.1.call-update) | async-done | bytes 524304 | tf_op jit(solution)/shard_map/psum | solution.py:85
  256.5 1.9 multiply_reduce_fusion
  260.6 128.7 %while.17 = (s32[]{:T(128)}, f32[128,2,64]{0,2,1:T(8,128)S(1)}, f32[4,512,128]{2,1,0:T(8,128)}, f32[4,512,128]{2,1,0:T(8,128)}, s32[4]{0:T(128)S(1)}, /*index=5*...) while((s32[]{:T(128)}, f32[128,2,64]{0,2,1:T(8,128)S(1)}, ...), condition=%wide.region_13.14_spmd.clone, body=%wide.region_12.13_spmd.clone.sunk | while | flops 169302016 | bytes 6349741 | solution.py:205
  264.4 4.4 compare_select_fusion.28
  269.6 15.6 %fusion.139 = (s32[512]{0:T(512)S(1)}, s32[512]{0:T(512)S(1)}) fusion(s32[]{:T(128)} %bitcast.254, pred[512]{0:T(512)(128)(4,1)S(1)} %compare_reduce_fusion.75, pred[512]{0:T(512)(128)(4,1)S(1)} %compare_reduce_fusion.76, pred[512]{0:T(512)(128)(4,1)S(1)} %compare_reduce_fusion.77, pred[512]{0:T(512)(128)(4,1)S(1)} %compare_reduce_fusion.78, ...), kind=kLoop, calls=%fused_computation.63.clone.1 | loop fusion | flops 19968 | bytes 19048 | tf_op jit(solution)/shard_map/while/body/eval_jaxpr/add | solution.py:89
  285.2 3.1 gather_fusion
  296.5 4.4 compare_select_fusion.28
  301.7 15.6 %fusion.139 = (s32[512]{0:T(512)S(1)}, s32[512]{0:T(512)S(1)}) fusion(s32[]{:T(128)} %bitcast.254, pred[512]{0:T(512)(128)(4,1)S(1)} %compare_reduce_fusion.75, pred[512]{0:T(512)(128)(4,1)S(1)} %compare_reduce_fusion.76, pred[512]{0:T(512)(128)(4,1)S(1)} %compare_reduce_fusion.77, pred[512]{0:T(512)(128)(4,1)S(1)} %compare_reduce_fusion.78, ...), kind=kLoop, calls=%fused_computation.63.clone.1 | loop fusion | flops 19968 | bytes 19048 | tf_op jit(solution)/shard_map/while/body/eval_jaxpr/add | solution.py:89
  317.4 3.1 gather_fusion
  328.7 4.4 compare_select_fusion.28
  333.9 15.6 %fusion.139 = (s32[512]{0:T(512)S(1)}, s32[512]{0:T(512)S(1)}) fusion(s32[]{:T(128)} %bitcast.254, pred[512]{0:T(512)(128)(4,1)S(1)} %compare_reduce_fusion.75, pred[512]{0:T(512)(128)(4,1)S(1)} %compare_reduce_fusion.76, pred[512]{0:T(512)(128)(4,1)S(1)} %compare_reduce_fusion.77, pred[512]{0:T(512)(128)(4,1)S(1)} %compare_reduce_fusion.78, ...), kind=kLoop, calls=%fused_computation.63.clone.1 | loop fusion | flops 19968 | bytes 19048 | tf_op jit(solution)/shard_map/while/body/eval_jaxpr/add | solution.py:89
  349.5 3.1 gather_fusion
  360.9 4.4 compare_select_fusion.28
  366.0 15.6 %fusion.139 = (s32[512]{0:T(512)S(1)}, s32[512]{0:T(512)S(1)}) fusion(s32[]{:T(128)} %bitcast.254, pred[512]{0:T(512)(128)(4,1)S(1)} %compare_reduce_fusion.75, pred[512]{0:T(512)(128)(4,1)S(1)} %compare_reduce_fusion.76, pred[512]{0:T(512)(128)(4,1)S(1)} %compare_reduce_fusion.77, pred[512]{0:T(512)(128)(4,1)S(1)} %compare_reduce_fusion.78, ...), kind=kLoop, calls=%fused_computation.63.clone.1 | loop fusion | flops 19968 | bytes 19048 | tf_op jit(solution)/shard_map/while/body/eval_jaxpr/add | solution.py:89
  381.7 3.1 gather_fusion
  391.9 66.8 %reduce-scatter.5.cloned.1.call-done = f32[128,128]{1,0:T(8,128)} async-done(((f32[2048,128]{1,0:T(8,128)}), f32[128,128]{1,0:T(8,128)}) %reduce-scatter.5.cloned.1.call-update) | async-done | bytes 65552 | tf_op jit(solution)/shard_map/reduce_scatter | solution.py:214
  459.6 69.8 %reduce-scatter.3.cloned.1.call-done = f32[128,128]{1,0:T(8,128)} async-done(((f32[2048,128]{1,0:T(8,128)}), f32[128,128]{1,0:T(8,128)}) %reduce-scatter.3.cloned.1.call-update) | async-done | bytes 65552 | tf_op jit(solution)/shard_map/reduce_scatter | solution.py:213
  530.2 2.3 convolution_bitcast_fusion
  538.5 67.6 %all-reduce.12.cloned.1.call-done = (f32[128,1024]{1,0:T(8,128)}, f32[128,1024]{1,0:T(8,128)}) async-done(((f32[128,1024]{1,0:T(8,128)}, f32[128,1024]{1,0:T(8,128)}), (f32[128,1024]{1,0:T(8,128)}, f32[128,1024]{1,0:T(8,128)})) %all-reduce.12.cloned.1.call-update) | async-done | bytes 1048592 | tf_op jit(solution)/shard_map/psum | solution.py:85
  608.9 2.2 fusion.66
  611.0 64.8 %all-reduce.1 = (bf16[1024]{0:T(1024)(128)(2,1)S(1)}, bf16[1024]{0:T(1024)(128)(2,1)S(1)}, bf16[2,128]{1,0:T(2,128)(2,1)S(1)}, bf16[1024]{0:T(1024)(128)(2,1)S(1...) all-reduce(bf16[1024]{0:T(1024)(128)(2,1)S(1)} %get-tuple-element.2, ...), channel_id=1, replica_groups=mesh['ctx'=16,'wa'=8] {'ctx'}, use_global_device_ids=true, to_apply=%region_20.21 | all-reduce | flops 6912 | bytes 27648 | tf_op jit(solution)/shard_map/psum | solution.py:236
  681.3 80.3 %all-reduce.14.cloned.1.call-done = (bf16[1024,3,128]{2,0,1:T(8,128)(2,1)}, bf16[128,1024]{1,0:T(8,128)(2,1)}, bf16[1024,512]{1,0:T(8,128)(2,1)}, bf16[512,1024]{1,0:T(8,128)(2,1)}) async-done(((bf16[1024,3,128]{2,0,1:T(8,128)(2,1)}, bf16[128,1024]{1,0:T(8,128)(2,1)}, bf16[1024,512]{1,0:T(8,128)(2,1)}, bf16[512,1024]{1,0:T(8,128)(2,1)}), (bf16[1024,3,128]{2,0,1:T(8,128)(2,1)}, bf16[128,1024]{1,0:T(8,128)(2,1)}, ...) | async-done | bytes 3145744 | tf_op jit(solution)/shard_map/psum | solution.py:238
  761.6 2.5 convert_element_type.205
  (392 shorter events, 73.9 us)
Async XLA Ops:
  7.2 171.6 %copy-start = (bf16[1024,512]{1,0:T(8,128)(2,1)S(1)}, bf16[1024,512]{1,0:T(8,128)(2,1)}, u32[]{:S(2)}) copy-start(bf16[1024,512]{1,0:T(8,128)(2,1)} %param.30) | copy-start | bytes 3145732
  7.2 5.2 copy-start.3
  7.2 6.9 copy-start.2
  7.2 9.6 %copy-start.46 = (bf16[2,128]{1,0:T(2,128)(2,1)S(1)}, bf16[2,128]{1,0:T(2,128)(2,1)}, u32[]{:S(2)}) copy-start(bf16[2,128]{1,0:T(2,128)(2,1)} %param.25) | copy-start | bytes 1540
  7.2 170.1 %all-reduce.8.cloned.1.call-start = ((), (), s32[]{:S(2)}) async-start(), calls=%async_computation.2 | async-start | bytes 1048576 | tf_op jit(solution)/shard_map/psum | solution.py:85
  8.8 57.0 %copy-start.1 = (s32[2048]{0:T(1024)S(1)}, s32[2048]{0:T(1024)}, u32[]{:S(2)}) copy-start(s32[2048]{0:T(1024)} %param.20) | copy-start | bytes 24580
  9.5 68.1 %copy-start.22 = (f32[1024]{0:T(1024)}, f32[1024]{0:T(1024)S(1)}, u32[]{:S(2)}) copy-start(f32[1024]{0:T(1024)S(1)} %convert_element_type.176) | copy-start | bytes 12292
  11.2 66.3 %copy-start.26 = (f32[128]{0:T(128)}, f32[128]{0:T(128)S(1)}, u32[]{:S(2)}) copy-start(f32[128]{0:T(128)S(1)} %broadcast_multiply_fusion.1) | copy-start | bytes 1540
  12.4 65.2 %copy-start.44 = (f32[128]{0:T(128)}, f32[128]{0:T(128)S(1)}, u32[]{:S(2)}) copy-start(f32[128]{0:T(128)S(1)} %fusion.33) | copy-start | bytes 1540
  12.4 65.1 %copy-start.34 = (f32[128]{0:T(128)}, f32[128]{0:T(128)S(1)}, u32[]{:S(2)}) copy-start(f32[128]{0:T(128)S(1)} %fusion.61) | copy-start | bytes 1540
  104.2 4.7 copy-start.4
  108.8 147.8 %all-reduce.10.cloned.1.call-start = ((), (), s32[]{:S(2)}) async-start(), calls=%async_computation.3 | async-start | bytes 1048576 | tf_op jit(solution)/shard_map/psum | solution.py:85
  108.9 71.7 %copy-start.24 = (f32[1024]{0:T(1024)}, f32[1024]{0:T(1024)S(1)}, u32[]{:S(2)}) copy-start(f32[1024]{0:T(1024)S(1)} %convert_element_type.185) | copy-start | bytes 12292
  108.9 149.5 %copy-start.19 = (f32[1024]{0:T(1024)}, f32[1024]{0:T(1024)S(1)}, u32[]{:S(2)}) copy-start(f32[1024]{0:T(1024)S(1)} %convert_element_type.184) | copy-start | bytes 12292
  178.6 79.9 %copy-start.30 = (f32[128]{0:T(128)}, f32[128]{0:T(128)S(1)}, u32[]{:S(2)}) copy-start(f32[128]{0:T(128)S(1)} %broadcast_multiply_fusion) | copy-start | bytes 1540
  178.8 79.7 %copy-start.36 = (f32[128]{0:T(128)}, f32[128]{0:T(128)S(1)}, u32[]{:S(2)}) copy-start(f32[128]{0:T(128)S(1)} %fusion.62) | copy-start | bytes 1540
  180.6 79.2 %copy-start.12 = (bf16[128,1024]{1,0:T(8,128)(2,1)S(1)}, bf16[128,1024]{1,0:T(8,128)(2,1)}, u32[]{:S(2)}) copy-start(bf16[128,1024]{1,0:T(8,128)(2,1)} %param.26) | copy-start | bytes 786436
  180.6 79.2 %copy-start.21 = (f32[128,2,64]{0,2,1:T(8,128)S(1)}, f32[128,2,64]{0,2,1:T(8,128)}, u32[]{:S(2)}) copy-start(f32[128,2,64]{0,2,1:T(8,128)} %get-tuple-element.391) | copy-start | bytes 196612
  181.9 276.8 %reduce-scatter.5.cloned.1.call-start = ((), (), s32[]{:S(2)}) async-start(), calls=%async_computation.5 | async-start | bytes 1114112 | tf_op jit(solution)/shard_map/reduce_scatter | solution.py:214
  389.3 140.1 %reduce-scatter.3.cloned.1.call-start = ((), (), s32[]{:S(2)}) async-start(), calls=%async_computation.4 | async-start | bytes 1114112 | tf_op jit(solution)/shard_map/reduce_scatter | solution.py:213
  389.8 216.3 %all-reduce.12.cloned.1.call-start = ((), (), s32[]{:S(2)}) async-start(), calls=%async_computation.6 | async-start | bytes 2097152 | tf_op jit(solution)/shard_map/psum | solution.py:85
  391.9 142.2 %copy-start.16 = (bf16[128,512]{1,0:T(8,128)(2,1)S(1)}, bf16[128,512]{1,0:T(8,128)(2,1)}, u32[]{:S(2)}) copy-start(bf16[128,512]{1,0:T(8,128)(2,1)} %copy-done.15) | copy-start | bytes 393220
  391.9 142.2 %copy-start.20 = (f32[1024]{0:T(1024)S(1)}, f32[1024]{0:T(1024)}, u32[]{:S(2)}) copy-start(f32[1024]{0:T(1024)} %copy-done.19) | copy-start | bytes 12292
  391.9 142.2 %copy-start.25 = (f32[1024]{0:T(1024)S(1)}, f32[1024]{0:T(1024)}, u32[]{:S(2)}) copy-start(f32[1024]{0:T(1024)} %copy-done.24) | copy-start | bytes 12292
  391.9 142.2 %copy-start.31 = (f32[128]{0:T(128)S(1)}, f32[128]{0:T(128)}, u32[]{:S(2)}) copy-start(f32[128]{0:T(128)} %copy-done.30) | copy-start | bytes 1540
  391.9 142.2 %copy-start.37 = (f32[128]{0:T(128)S(1)}, f32[128]{0:T(128)}, u32[]{:S(2)}) copy-start(f32[128]{0:T(128)} %copy-done.36) | copy-start | bytes 1540
  532.6 229.1 %all-reduce.14.cloned.1.call-start = ((), (), s32[]{:S(2)}) async-start(), calls=%async_computation.7 | async-start | bytes 6291456 | tf_op jit(solution)/shard_map/psum | solution.py:238
  538.2 69.2 %copy-start.45 = (f32[128]{0:T(128)S(1)}, f32[128]{0:T(128)}, u32[]{:S(2)}) copy-start(f32[128]{0:T(128)} %copy-done.44) | copy-start | bytes 1540
  538.2 72.8 %copy-start.28 = (bf16[1024]{0:T(1024)(128)(2,1)S(1)}, bf16[1024]{0:T(1024)(128)(2,1)}, u32[]{:S(2)}) copy-start(bf16[1024]{0:T(1024)(128)(2,1)} %get-tuple-element.255) | copy-start | bytes 6148
  538.3 72.8 %copy-start.29 = (bf16[1024]{0:T(1024)(128)(2,1)S(1)}, bf16[1024]{0:T(1024)(128)(2,1)}, u32[]{:S(2)}) copy-start(bf16[1024]{0:T(1024)(128)(2,1)} %get-tuple-element.259) | copy-start | bytes 6148
  538.3 72.8 %copy-start.43 = (bf16[512]{0:T(512)(128)(2,1)S(1)}, bf16[512]{0:T(512)(128)(2,1)}, u32[]{:S(2)}) copy-start(bf16[512]{0:T(512)(128)(2,1)} %get-tuple-element.308) | copy-start | bytes 3076
  606.1 74.4 %copy-start.14 = (f32[128,1024]{1,0:T(8,128)S(1)}, f32[128,1024]{1,0:T(8,128)}, u32[]{:S(2)}) copy-start(f32[128,1024]{1,0:T(8,128)} %get-tuple-element.292) | copy-start | bytes 1572868
  (29 other events, 79.5 us)
Sparse Core Ops, SparseCore 0:
  108.9 68.4 all-reduce.7
  182.0 74.4 all-reduce.9
  389.4 69.2 reduce-scatter.4
  463.5 65.8 reduce-scatter.2
  532.6 73.4 all-reduce.11
  609.9 151.6 all-reduce.13
where the time goes:
time: 778 us; the launch traced here: 775 us
  waiting for transfers between devices  427 us (55%)
  other arithmetic  135 us (17%)
  blocking collectives  115 us (15%)
  local copies, waits for them, and re-layouts  51 us (7%)
  matrix products  27.9 us (4%)
  between operations  14.9 us (2%)
    psum x3, waiting for transfers between devices, row_total(): lax.psum(jnp.einsum(pattern, left, right, preferred_element_type=jnp.floa...  210 us
    psum x1, waiting for transfers between devices, body(): lax.psum(grad_w_qkv.astype(jnp.bfloat16), 'ctx').astype(jnp.float32)  80.3 us
    add x6, other arithmetic, block_positions(): block_order[row_index // block_rows] * block_rows + row_index % block_rows  78.2 us
    reduce_scatter x1, waiting for transfers between devices, body(): lax.psum_scatter(key_terms_all, 'ctx', scatter_dimension=0, tiled=True)  69.8 us
    reduce_scatter x1, waiting for transfers between devices, body(): lax.psum_scatter(value_terms_all, 'ctx', scatter_dimension=0, tiled=True)  66.8 us
    psum x1, blocking collectives, body(): lax.psum(grad_ln1_gain.astype(jnp.bfloat16), 'ctx').astype(jnp.float32)  64.8 us
    all_gather x1, blocking collectives, body(): key_piece = lax.all_gather(keys_local, 'ctx', axis=0, tiled=True)  28.5 us
    gather x131, other arithmetic, block_positions(): block_order[row_index // block_rows] * block_rows + row_index % block_rows  27.1 us
  transfers between devices with their start and end apart: 6, of which 6 were waited for; matrix products, arithmetic and copies ran while one was open for 2% of the time, Pallas kernels for 0%

commit v1 on v0

v1 whole, which is shorter than its diff:
```python
import jax
import jax.numpy as jnp
from jax import lax
from jax.experimental import pallas as pl
from jax.experimental.pallas import tpu as pltpu
from jax.sharding import PartitionSpec as P

F32 = jnp.float32
BF = jnp.bfloat16
MESH = pl.DeviceIdType.MESH
GELU_A = 0.7978845608028654
GELU_B = 0.044715

(
    KV,
    KVF,
    RS1,
    AGC,
    RS2,
    RS3,
    AGD,
    AGY,
    CMB,
    RKV,
    RA,
    AGA,
    FWA,
    RB,
    AGB,
    FWB,
    RC,
    AGCC,
    FWC,
    RS4,
    RS5,
    AGG,
    AGV,
    NSEM,
) = range(24)


def nn(a, b):
    return lax.dot_general(a, b, (((1,), (0,)), ((), ())), preferred_element_type=F32)


def nt(a, b):
    return lax.dot_general(a, b, (((1,), (1,)), ((), ())), preferred_element_type=F32)


def tn(a, b):
    return lax.dot_general(a, b, (((0,), (0,)), ((), ())), preferred_element_type=F32)


def normalize(rows):
    centered = rows - jnp.mean(rows, -1, keepdims=True)
    rstd = lax.rsqrt(jnp.mean(centered * centered, -1, keepdims=True) + 1e-05)
    return centered * rstd, rstd


def norm_back(grad, gain, xhat, rstd):
    gx = grad * gain
    return rstd * (
        gx - jnp.mean(gx, -1, keepdims=True) - xhat * jnp.mean(gx * xhat, -1, keepdims=True)
    )


def kernel(
    order_ref,
    seg_ref,
    x_ref,
    g_ref,
    vec_ref,
    wqkv_hbm,
    wout_hbm,
    wup_hbm,
    wdn_hbm,
    y_out,
    gin_out,
    gup_out,
    gdn_out,
    gwo_out,
    gqkv_out,
    vec_out,
    ctx_out,
    wqkv,
    wout,
    wup,
    wdn,
    load_sem,
    xhat_all,
    normed,
    kv,
    q2,
    scores,
    acc,
    attn_t,
    attn_low,
    rs1s,
    rs1r,
    c_all,
    dm,
    rs2s,
    rs2r,
    rs3s,
    rs3r,
    dh_all,
    y_all,
    dkv,
    pkv,
    rkv,
    ga,
    pa,
    ra,
    oa,
    gb,
    pb,
    rb,
    ob,
    gc,
    pc,
    rc,
    oc,
    rs4s,
    rs4r,
    g_all,
    vs,
    vr,
    vall,
    cvs,
    cvr,
    ss,
    rs,
    cs_s,
    cs_r,
):
    ctx = lax.axis_index("ctx")
    wa = lax.axis_index("wa")
    core = lax.rem(ctx, 2)
    chip = lax.div(ctx, 2)
    other = 1 - core
    slot = core * 8 + chip
    partner = chip * 2 + other

    def to_wa(src, dst, kind, d):
        return pltpu.make_async_remote_copy(
            src_ref=src,
            dst_ref=dst,
            send_sem=ss.at[kind, d],
            recv_sem=rs.at[kind, d],
            device_id={"wa": lax.rem(wa + d, 8)},
            device_id_type=MESH,
        )

    def to_chip(src, dst, kind, d):
        return pltpu.make_async_remote_copy(
            src_ref=src,
            dst_ref=dst,
            send_sem=ss.at[kind, d],
            recv_sem=rs.at[kind, d],
            device_id={"ctx": lax.rem(chip + d, 8) * 2 + core},
            device_id_type=MESH,
        )

    def to_partner(src, dst, kind, d):
        return pltpu.make_async_remote_copy(
            src_ref=src,
            dst_ref=dst,
            send_sem=ss.at[kind, d],
            recv_sem=rs.at[kind, d],
            device_id={"ctx": partner},
            device_id_type=MESH,
        )

    def each(low, high, step):
        @pl.loop(low, high)
        def _(d):
            step(d)

    barrier = pltpu.get_barrier_semaphore()
    each(
        1,
        16,
        lambda d: pl.semaphore_signal(
            barrier, inc=1, device_id={"ctx": lax.rem(ctx + d, 16)}, device_id_type=MESH
        ),
    )
    each(
        1,
        8,
        lambda d: pl.semaphore_signal(
            barrier, inc=1, device_id={"wa": lax.rem(wa + d, 8)}, device_id_type=MESH
        ),
    )

    loads = [
        pltpu.make_async_copy(
            wqkv_hbm.at[i], wqkv.at[:, pl.ds(128 * i, 128)], load_sem.at[i]
        )
        for i in range(3)
    ] + [
        pltpu.make_async_copy(wdn_hbm, wdn, load_sem.at[3]),
        pltpu.make_async_copy(wout_hbm, wout, load_sem.at[4]),
        pltpu.make_async_copy(wup_hbm, wup, load_sem.at[5]),
    ]
    for load in loads:
        load.start()

    ln1_gain = vec_ref[0:1, :]
    ln1_bias = vec_ref[1:2, :]
    b_out = vec_ref[2:3, :]
    ln2_gain = vec_ref[3:4, :]
    ln2_bias = vec_ref[4:5, :]
    b_down = vec_ref[5:6, :]
    b_up = vec_ref[6:7, 0:512]
    b_q = vec_ref[7:8, 0:128]
    b_v = vec_ref[7:8, 128:256]

    xhat, _ = normalize(x_ref[...].astype(F32))
    xhat_all[...] = xhat
    normed[...] = (xhat * ln1_gain + ln1_bias).astype(BF)
    for i in range(3):
        loads[i].wait()
    proj = nn(normed[...], wqkv[...])
    kv[slot, :, 0:128] = proj[:, 128:256].astype(BF)
    kv[slot, :, 128:256] = (proj[:, 256:384] + b_v).astype(BF)
    pl.semaphore_wait(barrier, 22)

    to_partner(kv.at[slot], kv.at[slot], KV, 0).start()
    each(1, 8, lambda d: to_chip(kv.at[slot], kv.at[slot], KV, d).start())

    q_low = (proj[:, 0:128] + b_q).astype(BF) * jnp.asarray(0.125, BF)
    lane = lax.broadcasted_iota(jnp.int32, (128, 128), 1)
    zero = jnp.zeros((128, 128), BF)
    q2[0:128, :] = jnp.where(lane < 64, q_low, zero)
    q2[128:256, :] = jnp.where(lane >= 64, q_low, zero)

    lanes = lax.broadcasted_iota(jnp.int32, (1, 256), 1)
    lanes = jnp.where(lanes >= 128, lanes - 128, lanes)
    q_pos = jnp.where(
        lanes < 64, lanes + 64 * order_ref[2 * ctx], lanes - 64 + 64 * order_ref[2 * ctx + 1]
    )
    seg = seg_ref[...]
    one = jnp.ones(seg.shape, F32)
    none = jnp.zeros(seg.shape, F32)

    def count(test):
        part = jnp.sum(jnp.where(test, one, none), axis=0, keepdims=True)
        return jnp.sum(part, axis=1, keepdims=True)

    first_end = count(seg < 1)
    second_end = count(seg < 2)
    q_float = q_pos.astype(F32)
    q_first = jnp.where(
        q_float >= second_end,
        second_end,
        jnp.where(q_float >= first_end, first_end, jnp.zeros_like(q_float)),
    ).astype(jnp.int32)
    row = lax.broadcasted_iota(jnp.int32, (128, 256), 0)

    def score(s, top):
        keys = kv[s, :, 0:128]
        owner = 2 * lax.rem(s, 8) + lax.div(s, 8)
        k_pos = jnp.where(
            row < 64, row + 64 * order_ref[2 * owner], row - 64 + 64 * order_ref[2 * owner + 1]
        )
        allowed = (k_pos <= q_pos) & (k_pos >= q_first)
        masked = jnp.where(allowed, nt(keys, q2[...]), -1e30)
        scores[s] = masked
        return jnp.maximum(top, jnp.max(masked.reshape(16, 8, 256), axis=0))

    loads[3].wait()
    dm[...] = nt(g_ref[...], wdn[...])

    top = score(slot, jnp.full((8, 256), -1e30, F32))
    to_partner(kv.at[slot], kv.at[slot], KV, 0).wait_recv()
    top = score(other * 8 + chip, top)

    def near(d, top):
        s = core * 8 + lax.rem(chip + 8 - d, 8)
        to_chip(kv.at[slot], kv.at[s], KV, d).wait_recv()
        to_partner(kv.at[s], kv.at[s], KVF, d).start()
        return score(s, top)

    top = lax.fori_loop(1, 8, near, top)

    def far(d, top):
        s = other * 8 + lax.rem(chip + 8 - d, 8)
        to_partner(kv.at[s], kv.at[s], KVF, d).wait_recv()
        return score(s, top)

    top = lax.fori_loop(1, 8, far, top)

    top = jnp.max(top, axis=0, keepdims=True)
    acc[...] = jnp.zeros_like(acc)

    def mix(s, total):
        p = jnp.exp(scores[s] - top)
        acc[...] += tn(kv[s, :, 128:256], p.astype(BF))
        return total + jnp.sum(p.reshape(16, 8, 256), axis=0)

    total = lax.fori_loop(0, 16, mix, jnp.zeros((8, 256), F32))
    total = jnp.sum(total, axis=0, keepdims=True)
    lse = top + jnp.log(total)
    half = lax.broadcasted_iota(jnp.int32, (128, 128), 0) < 64

    def diagonal(both):
        return jnp.where(half, both[:, 0:128], both[:, 128:256])

    raw_t = diagonal(acc[...] / total)
    attn_t[...] = raw_t
    attn_low[...] = raw_t.T.astype(BF)

    def reduce_start(part, send, recv, kind):
        send[...] = part.astype(BF).reshape(8, 16, 1024)
        each(1, 8, lambda d: to_wa(send.at[lax.rem(wa + d, 8)], recv.at[d], kind, d).start())

    def reduce_end(send, recv, kind):
        each(1, 8, lambda d: to_wa(send.at[lax.rem(wa + d, 8)], recv.at[d], kind, d).wait_recv())
        whole = send[wa].astype(F32)
        for d in range(1, 8):
            whole = whole + recv[d].astype(F32)
        return whole

    def gather_start(buf, kind):
        each(1, 8, lambda d: to_wa(buf.at[wa], buf.at[wa], kind, d).start())

    def gather_end(buf, kind):
        each(
            1,
            8,
            lambda d: to_wa(buf.at[wa], buf.at[lax.rem(wa + 8 - d, 8)], kind, d).wait_recv(),
        )

    loads[4].wait()
    reduce_start(nn(attn_low[...], wout[...]), rs1s, rs1r, RS1)
    mine = pl.ds(pl.multiple_of(wa * 16, 16), 16)
    x_mine = x_ref[mine, :].astype(F32)
    g_mine = g_ref[mine, :].astype(F32)
    hidden = x_mine + reduce_end(rs1s, rs1r, RS1) + b_out
    hat_two, rstd_two = normalize(hidden)
    c_all[wa] = (hat_two * ln2_gain + ln2_bias).astype(BF)
    gather_start(c_all, AGC)
    loads[5].wait()
    gather_end(c_all, AGC)

    c_low = c_all[...].reshape(128, 1024)
    up = nn(c_low, wup[...]) + b_up
    tanh = jnp.tanh(GELU_A * (up + GELU_B * up * up * up))
    slope = 0.5 * (1.0 + tanh) + 0.5 * up * (1.0 - tanh * tanh) * GELU_A * (
        1.0 + 3.0 * GELU_B * up * up
    )
    du = (dm[...] * slope).astype(BF)
    act = (0.5 * up * (1.0 + tanh)).astype(BF)
    reduce_start(nt(du, wup[...]), rs2s, rs2r, RS2)
    reduce_start(nn(act, wdn[...]), rs3s, rs3r, RS3)
    ga[:, 0:64, :] = tn(c_low, du).astype(BF).reshape(16, 64, 512)
    down = tn(act, g_ref[...]).astype(BF)
    ga[:, 64:96, :] = down[:, 0:512].reshape(16, 32, 512)
    ga[:, 96:128, :] = down[:, 512:1024].reshape(16, 32, 512)

    def combine(buf, kept, index):
        return pltpu.make_async_remote_copy(
            src_ref=buf.at[pl.ds(pl.multiple_of(other * 8, 8), 8)],
            dst_ref=kept,
            send_sem=cs_s.at[index],
            recv_sem=cs_r.at[index],
            device_id={"ctx": partner},
            device_id_type=MESH,
        )

    def combined(buf, kept, index):
        combine(buf, kept, index).wait_recv()

        @pl.loop(0, 8)
        def _(j):
            buf[core * 8 + j] = (buf[core * 8 + j].astype(F32) + kept[j].astype(F32)).astype(BF)

    def scatter_start(buf, recv, kind):
        each(
            1,
            8,
            lambda d: to_chip(
                buf.at[core * 8 + lax.rem(chip + d, 8)], recv.at[d], kind, d
            ).start(),
        )

    def scatter_end(buf, recv, kind):
        each(
            1,
            8,
            lambda d: to_chip(
                buf.at[core * 8 + lax.rem(chip + d, 8)], recv.at[d], kind, d
            ).wait_recv(),
        )
        whole = buf[slot].astype(F32)
        for d in range(1, 8):
            whole = whole + recv[d].astype(F32)
        return whole.astype(BF)

    def spread_start(buf, kind):
        to_partner(buf.at[slot], buf.at[slot], kind, 0).start()
        each(1, 8, lambda d: to_chip(buf.at[slot], buf.at[slot], kind, d).start())

    def spread_pass(buf, kind, forward):
        def step(d):
            s = core * 8 + lax.rem(chip + 8 - d, 8)
            to_chip(buf.at[slot], buf.at[s], kind, d).wait_recv()
            to_partner(buf.at[s], buf.at[s], forward, d).start()

        each(1, 8, step)

    def spread_end(buf, kind, forward):
        s = other * 8 + chip
        to_partner(buf.at[s], buf.at[s], kind, 0).wait_recv()

        def step(d):
            t = other * 8 + lax.rem(chip + 8 - d, 8)
            to_partner(buf.at[t], buf.at[t], forward, d).wait_recv()

        each(1, 8, step)

    combine(ga, pa, 0).start()

    def vec_row(r, value):
        for j in range(8):
            vs[j, r : r + 1, :] = value[:, 128 * j : 128 * j + 128]

    def rows_sum(value):
        return jnp.sum(value, axis=0, keepdims=True)

    sum_up = rows_sum(du.astype(F32))
    for j in range(4):
        cvs[8 + j : 9 + j, :] = sum_up[:, 128 * j : 128 * j + 128]

    dc = reduce_end(rs2s, rs2r, RS2)
    d_hidden = g_mine + norm_back(dc, ln2_gain, hat_two, rstd_two)
    dh_all[wa] = d_hidden.astype(BF)
    gather_start(dh_all, AGD)
    combined(ga, pa, 0)
    scatter_start(ga, ra, RA)
    vec_row(0, rows_sum(dc * hat_two))
    vec_row(1, rows_sum(dc))
    vec_row(2, rows_sum(d_hidden))
    vec_row(3, rows_sum(g_mine))
    y_all[wa] = (hidden + reduce_end(rs3s, rs3r, RS3) + b_down).astype(BF)
    gather_start(y_all, AGY)
    gather_end(dh_all, AGD)

    dh_low = dh_all[...].reshape(128, 1024)
    d_attn = nt(dh_low, wout[...]).astype(BF)
    dot_t = d_attn.astype(F32).T * attn_t[...]
    delta = jnp.concatenate(
        [
            jnp.sum(dot_t[0:64], axis=0, keepdims=True),
            jnp.sum(dot_t[64:128], axis=0, keepdims=True),
        ],
        axis=1,
    )
    do2 = jnp.concatenate(
        [jnp.where(lane < 64, d_attn, zero), jnp.where(lane >= 64, d_attn, zero)], axis=0
    )
    acc[...] = jnp.zeros_like(acc)

    def back(s):
        p = jnp.exp(scores[s] - lse)
        ds = (p * (nt(kv[s, :, 128:256], do2) - delta)).astype(BF)
        acc[...] += tn(kv[s, :, 0:128], ds)
        dkv[s, :, 0:128] = nn(ds, q2[...]).astype(BF)
        dkv[s, :, 128:256] = nn(p.astype(BF), do2).astype(BF)

    each(0, 8, lambda j: back(other * 8 + j))
    combine(dkv, pkv, 1).start()
    each(0, 8, lambda j: back(core * 8 + j))
    combined(dkv, pkv, 1)
    scatter_start(dkv, rkv, RKV)

    dq = (diagonal(acc[...]) * 0.125).T.astype(BF)
    gb[:, 64:128, :] = tn(normed[...], dq).astype(BF).reshape(16, 64, 128)
    d_out = tn(attn_low[...], dh_low).astype(BF)
    for s in range(16):
        gb[s, 0:64, :] = d_out[64 * (s % 2) : 64 * (s % 2) + 64, 128 * (s // 2) : 128 * (s // 2) + 128]
    combine(gb, pb, 2).start()

    oa[slot] = scatter_end(ga, ra, RA)
    spread_start(oa, AGA)
    combined(gb, pb, 2)
    scatter_start(gb, rb, RB)

    dkv_mine = scatter_end(dkv, rkv, RKV)
    d_qkv = jnp.concatenate([dq, dkv_mine], axis=1)
    da = nt(d_qkv, wqkv[...])
    reduce_start(da, rs4s, rs4r, RS4)
    both = tn(normed[...], dkv_mine).astype(BF)
    gc[:, 0:64, :] = both[:, 0:128].reshape(16, 64, 128)
    gc[:, 64:128, :] = both[:, 128:256].reshape(16, 64, 128)
    combine(gc, pc, 3).start()
    vec_row(4, rows_sum(da * xhat_all[...]))
    vec_row(5, rows_sum(da))
    for j in range(8):
        vs[j, 6:8, :] = jnp.zeros((2, 128), F32)
    each(1, 8, lambda d: to_wa(vs.at[lax.rem(wa + d, 8)], vr.at[d], RS5, d).start())
    cvs[12:13, :] = rows_sum(dq.astype(F32))
    cvs[13:14, :] = rows_sum(dkv_mine[:, 128:256].astype(F32))
    cvs[14:16, :] = jnp.zeros((2, 128), F32)
    spread_pass(oa, AGA, FWA)
    combined(gc, pc, 3)
    scatter_start(gc, rc, RC)

    hat_one, rstd_one = normalize(x_mine)
    d_first = reduce_end(rs4s, rs4r, RS4)
    g_all[wa] = (d_hidden + norm_back(d_first, ln1_gain, hat_one, rstd_one)).astype(BF)
    gather_start(g_all, AGG)

    each(1, 8, lambda d: to_wa(vs.at[lax.rem(wa + d, 8)], vr.at[d], RS5, d).wait_recv())
    vec_sum = vs[wa]
    for d in range(1, 8):
        vec_sum = vec_sum + vr[d]
    cvs[0:8, :] = vec_sum
    cvr[ctx] = cvs[...]

    def to_ctx(dst, d):
        return pltpu.make_async_remote_copy(
            src_ref=cvs,
            dst_ref=cvr.at[dst],
            send_sem=cs_s.at[4 + d],
            recv_sem=cs_r.at[4 + d],
            device_id={"ctx": lax.rem(ctx + d, 16)},
            device_id_type=MESH,
        )

    each(1, 16, lambda d: to_ctx(ctx, d).start())
    ob[slot] = scatter_end(gb, rb, RB)
    spread_start(ob, AGB)
    oc[slot] = scatter_end(gc, rc, RC)
    spread_start(oc, AGCC)
    each(1, 16, lambda d: to_ctx(lax.rem(ctx + 16 - d, 16), d).wait_recv())
    ctx_sum = cvr[0]
    for i in range(1, 16):
        ctx_sum = ctx_sum + cvr[i]
    ctx_out[...] = ctx_sum[8:16, :]
    vall[wa] = ctx_sum[0:8, :]
    gather_start(vall, AGV)
    spread_pass(ob, AGB, FWB)
    spread_pass(oc, AGCC, FWC)

    spread_end(oa, AGA, FWA)
    gup_out[...] = oa[:, 0:64, :].reshape(1024, 512)
    gdn_out[:, 0:512] = oa[:, 64:96, :].reshape(512, 512)
    gdn_out[:, 512:1024] = oa[:, 96:128, :].reshape(512, 512)
    gather_end(y_all, AGY)
    y_out[...] = y_all[...].reshape(128, 1024)
    gather_end(g_all, AGG)
    gin_out[...] = g_all[...].reshape(128, 1024)
    spread_end(ob, AGB, FWB)
    for s in range(16):
        gwo_out[64 * (s % 2) : 64 * (s % 2) + 64, 128 * (s // 2) : 128 * (s // 2) + 128] = ob[
            s, 0:64, :
        ]
    gqkv_out[0] = ob[:, 64:128, :].reshape(1024, 128)
    spread_end(oc, AGCC, FWC)
    gqkv_out[1] = oc[:, 0:64, :].reshape(1024, 128)
    gqkv_out[2] = oc[:, 64:128, :].reshape(1024, 128)
    gather_end(vall, AGV)
    vec_out[...] = vall[...]

    for buf, kind, forward in ((kv, KV, KVF), (oa, AGA, FWA), (ob, AGB, FWB), (oc, AGCC, FWC)):
        to_partner(buf.at[slot], buf.at[slot], kind, 0).wait_send()

        def sent(d, buf=buf, kind=kind, forward=forward):
            to_chip(buf.at[slot], buf.at[slot], kind, d).wait_send()
            to_partner(buf.at[slot], buf.at[slot], forward, d).wait_send()

        each(1, 8, sent)
    for buf, kind in (
        (rs1s, RS1),
        (rs2s, RS2),
        (rs3s, RS3),
        (rs4s, RS4),
        (c_all, AGC),
        (dh_all, AGD),
        (y_all, AGY),
        (g_all, AGG),
        (vs, RS5),
        (vall, AGV),
    ):
        each(
            1,
            8,
            lambda d, buf=buf, kind=kind: to_wa(buf.at[wa], buf.at[wa], kind, d).wait_send(),
        )
    for buf, kind in ((ga, RA), (dkv, RKV), (gb, RB), (gc, RC)):
        each(
            1,
            8,
            lambda d, buf=buf, kind=kind: to_chip(
                buf.at[slot], buf.at[slot], kind, d
            ).wait_send(),
        )
    for index, (buf, kept) in enumerate(((ga, pa), (dkv, pkv), (gb, pb), (gc, pc))):
        combine(buf, kept, index).wait_send()
    each(1, 16, lambda d: to_ctx(ctx, d).wait_send())


def body(
    layer_input,
    block_order,
    seg_ids,
    cotangent,
    ln1_gain,
    ln1_bias,
    w_qkv,
    b_qv,
    w_out,
    b_out,
    ln2_gain,
    ln2_bias,
    w_up,
    b_up,
    w_down,
    b_down,
):
    vectors = jnp.stack(
        [
            ln1_gain,
            ln1_bias,
            b_out,
            ln2_gain,
            ln2_bias,
            b_down,
            jnp.pad(b_up, (0, 512)),
            jnp.pad(b_qv.reshape(256), (0, 768)),
        ]
    ).astype(F32)
    vmem = pl.BlockSpec(memory_space=pltpu.VMEM)
    smem = pl.BlockSpec(memory_space=pltpu.SMEM)
    hbm = pl.BlockSpec(memory_space=pl.ANY)

    def bf(*shape):
        return pltpu.VMEM(shape, BF)

    def f32(*shape):
        return pltpu.VMEM(shape, F32)

    outs = pl.pallas_call(
        kernel,
        out_shape=(
            jax.ShapeDtypeStruct((128, 1024), BF),
            jax.ShapeDtypeStruct((128, 1024), BF),
            jax.ShapeDtypeStruct((1024, 512), BF),
            jax.ShapeDtypeStruct((512, 1024), BF),
            jax.ShapeDtypeStruct((128, 1024), BF),
            jax.ShapeDtypeStruct((3, 1024, 128), BF),
            jax.ShapeDtypeStruct((8, 8, 128), F32),
            jax.ShapeDtypeStruct((8, 128), F32),
        ),
        in_specs=[smem, vmem, vmem, vmem, vmem, hbm, hbm, hbm, hbm],
        out_specs=(vmem,) * 8,
        scratch_shapes=[
            bf(1024, 384),
            bf(128, 1024),
            bf(1024, 512),
            bf(512, 1024),
            pltpu.SemaphoreType.DMA((6,)),
            f32(128, 1024),
            bf(128, 1024),
            bf(16, 128, 256),
            bf(256, 128),
            f32(16, 128, 256),
            f32(128, 256),
            f32(128, 128),
            bf(128, 128),
            bf(8, 16, 1024),
            bf(8, 16, 1024),
            bf(8, 16, 1024),
            f32(128, 512),
            bf(8, 16, 1024),
            bf(8, 16, 1024),
            bf(8, 16, 1024),
            bf(8, 16, 1024),
            bf(8, 16, 1024),
            bf(8, 16, 1024),
            bf(16, 128, 256),
            bf(8, 128, 256),
            bf(8, 128, 256),
            bf(16, 128, 512),
            bf(8, 128, 512),
            bf(8, 128, 512),
            bf(16, 128, 512),
            bf(16, 128, 128),
            bf(8, 128, 128),
            bf(8, 128, 128),
            bf(16, 128, 128),
            bf(16, 128, 128),
            bf(8, 128, 128),
            bf(8, 128, 128),
            bf(16, 128, 128),
            bf(8, 16, 1024),
            bf(8, 16, 1024),
            bf(8, 16, 1024),
            f32(8, 8, 128),
            f32(8, 8, 128),
            f32(8, 8, 128),
            f32(16, 128),
            f32(16, 16, 128),
            pltpu.SemaphoreType.DMA((NSEM, 8)),
            pltpu.SemaphoreType.DMA((NSEM, 8)),
            pltpu.SemaphoreType.DMA((20,)),
            pltpu.SemaphoreType.DMA((20,)),
        ],
        compiler_params=pltpu.CompilerParams(
            collective_id=0, has_side_effects=True, vmem_limit_bytes=56 << 20
        ),
        name="layer",
    )(
        block_order,
        seg_ids.reshape(16, 128),
        layer_input,
        cotangent,
        vectors,
        w_qkv.transpose(1, 0, 2),
        w_out,
        w_up,
        w_down,
    )
    y, gin, gup, gdn, gwo, gqkv, vec, ctx_vec = outs

    def whole(r):
        return vec[:, r, :].reshape(1024)

    return (
        y,
        gin.astype(F32),
        whole(4),
        whole(5),
        gqkv.astype(F32).transpose(1, 0, 2),
        ctx_vec[4:6, :],
        gwo.astype(F32),
        whole(2),
        whole(0),
        whole(1),
        gup.astype(F32),
        ctx_vec[0:4, :].reshape(512),
        gdn.astype(F32),
        whole(3),
    )


def solution(mesh):
    placed = (
        P("ctx", None),
        P(),
        P(),
        P("ctx", None),
        P(),
        P(),
        P(None, None, "wa"),
        P(None, "wa"),
        P("wa", None),
        P(),
        P(),
        P(),
        P(None, "wa"),
        P("wa"),
        P("wa", None),
        P(),
    )
    return jax.shard_map(
        body,
        mesh=mesh,
        in_specs=placed,
        out_specs=(
            P("ctx", None),
            P("ctx", None),
            P(),
            P(),
            P(None, None, "wa"),
            P(None, "wa"),
            P("wa", None),
            P(),
            P(),
            P(),
            P(None, "wa"),
            P("wa"),
            P("wa", None),
            P(),
        ),
        check_vma=False,
    )
```

time: 778 us -> 129 us (0.17)
  waiting for transfers between devices: 427 us -> 0 us
  other arithmetic: 135 us -> 7.95 us
  blocking collectives: 115 us -> 0 us
  Pallas kernels: 0 us -> 109 us
  local copies, waits for them, and re-layouts: 51 us -> 10.5 us
  matrix products: 27.9 us -> 0 us
  between operations: 14.9 us -> 0.68 us
    psum x4 -> x0, waiting for transfers between devices: 290 us -> none  [the longest x3 210 us: row_total(): lax.psum(jnp.einsum(pattern, left, right, preferred_element_type=jnp.floa...]
    reduce_scatter x2 -> x0, waiting for transfers between devices: 137 us -> none  [the longest x1 69.8 us: body(): lax.psum_scatter(key_terms_all, 'ctx', scatter_dimension=0, tiled=True)]
    pallas_call x0 -> x1, Pallas kernels: none -> 109 us  [body(): pl.pallas_call(kernel, out_shape=(jax.ShapeDtypeStruct((128, 1024), BF),...]
    add x9 -> x0, other arithmetic: 78.8 us -> none  [the longest x6 78.2 us: block_positions(): block_order[row_index // block_rows] * block_rows + row_index % block_rows]
    psum x1 -> x0, blocking collectives: 64.8 us -> none  [body(): lax.psum(grad_ln1_gain.astype(jnp.bfloat16), 'ctx').astype(jnp.float32)]
    all_gather x2 -> x0, blocking collectives: 50.6 us -> none  [the longest x1 28.5 us: body(): key_piece = lax.all_gather(keys_local, 'ctx', axis=0, tiled=True)]
    gather x17 -> x0, local copies, waits for them, and re-layouts: 33.9 us -> none  [the longest x4 12.6 us: key_step(): seg_ids[key_pos]]
    dot_general x34 -> x0, matrix products: 27.9 us -> none  [the longest x4 5.78 us: row_total(): jnp.einsum(pattern, left, right, preferred_element_type=jnp.float32)]
  transfers between devices with their start and end apart: 6 -> 0, of which waited for: 6 -> 0; matrix products, arithmetic and copies ran while one was open for 2% -> 0% of each run, Pallas kernels for 0% -> 0%
where the time goes in v1:
time: 129 us; the launch traced here: 128 us
  Pallas kernels  109 us (84%)
  local copies, waits for them, and re-layouts  10.5 us (8%)
  other arithmetic  7.95 us (6%)
    pallas_call x1, Pallas kernels, body(): pl.pallas_call(kernel, out_shape=(jax.ShapeDtypeStruct((128, 1024), BF),...  109 us
    another operation x9, local copies, waits for them, and re-layouts, body(): jnp.stack([ln1_gain, ln1_bias, b_out, ln2_gain, ln2_bias, b_down, jnp.pad...  4.19 us
    convert_element_type x1, other arithmetic, body(): gup.astype(F32)  2.83 us

profile of v1, /device:TPU:1, one launch (start us, length us, event | category | flops | bytes accessed | tf_op | source)
XLA Modules:
  0.0 128.2 jit_solution(6603782710154102890)
XLA Ops:
  0.6 0.7 pad.8
  1.3 0.7 pad.9
  2.0 0.7 stack.27
  2.7 0.7 stack.28
  3.4 0.7 stack.29
  4.1 0.7 stack.30
  4.8 0.7 stack.31
  5.4 0.7 stack.32
  6.1 0.1 stack.35
  6.2 0.6 convert_element_type.20.vec_ref
  6.8 109.1 %layer.1 = (bf16[128,1024]{1,0:T(8,128)(2,1)}, bf16[128,1024]{1,0:T(8,128)(2,1)}, bf16[1024,512]{1,0:T(8,128)(2,1)}, bf16[512,1024]{1,0:T(8,128)(2,1)}, bf16[128...) custom-call(s32[32]{0:T(128)} %order_ref.1, s32[16,128]{1,0:T(8,128)} %bitcast.14, ...), custom_call_target="tpu_custom_call" | custom-call | tf_op jit(solution)/shard_map/layer/pallas_call | solution.py:644
  115.9 0.0 copy-start
  115.9 1.7 %fusion = (f32[8,1,128]{2,1,0:T(1,128)}, f32[8,1,128]{2,1,0:T(1,128)}, f32[8,1,128]{2,1,0:T(1,128)}, f32[8,1,128]{2,1,0:T(1,128)}, f32[8,1,128]{2,1,0:T(1,128)}, /*index=5*/f32[8,1,128]{2,1,0:T(1,128)}) fusion(f32[8,8,128]{2,1,0:T(8,128)} %get-tuple-element.24), kind=kLoop, calls=%fused_computation.2 | loop fusion | bytes 49152 | tf_op jit(solution)/shard_map/slice | solution.py:728
  117.6 1.3 slice_bitcast_fusion
  118.9 1.2 slice.26
  120.1 2.8 %convert_element_type.23 = f32[1024,512]{1,0:T(8,128)} convert(bf16[1024,512]{1,0:T(8,128)(2,1)} %get-tuple-element.28) | non-fusion elementwise | flops 524288 | bytes 3145728 | tf_op jit(solution)/shard_map/convert_element_type | solution.py:741
  123.0 0.0 copy-start.1
  123.0 0.0 copy-done
  123.0 0.0 copy-start.3
  123.0 1.6 %convert_element_type.24 = f32[512,1024]{1,0:T(8,128)} convert(bf16[512,1024]{1,0:T(8,128)(2,1)S(1)} %copy-done) | non-fusion elementwise | flops 524288 | bytes 3145728 | tf_op jit(solution)/shard_map/convert_element_type | solution.py:743
  124.5 0.0 copy-start.2
  124.5 0.0 copy-start.4
  124.5 0.0 copy-done.1
  124.5 1.2 convert_bitcast_fusion
  125.8 0.0 copy-done.3
  125.8 0.8 convert_element_type.21
  126.6 0.0 copy-done.2
  126.6 0.8 convert_element_type.22
  127.5 0.0 copy-done.4
  127.5 0.7 copy.31
  (2 shorter events, 0.0 us)
Async XLA Ops:
  115.9 7.0 %copy-start = (bf16[512,1024]{1,0:T(8,128)(2,1)S(1)}, bf16[512,1024]{1,0:T(8,128)(2,1)}, u32[]{:S(2)}) copy-start(bf16[512,1024]{1,0:T(8,128)(2,1)} %get-tuple-element.29) | copy-start | bytes 3145732
  123.0 1.6 %copy-start.1 = (bf16[3,1024,128]{2,1,0:T(8,128)(2,1)S(1)}, bf16[3,1024,128]{2,1,0:T(8,128)(2,1)}, u32[]{:S(2)}) copy-start(bf16[3,1024,128]{2,1,0:T(8,128)(2,1)} %get-tuple-element.25) | copy-start | bytes 2359300
  123.0 2.8 %copy-start.3 = (bf16[128,1024]{1,0:T(8,128)(2,1)S(1)}, bf16[128,1024]{1,0:T(8,128)(2,1)}, u32[]{:S(2)}) copy-start(bf16[128,1024]{1,0:T(8,128)(2,1)} %get-tuple-element.23) | copy-start | bytes 786436
  124.5 2.1 %copy-start.2 = (bf16[128,1024]{1,0:T(8,128)(2,1)S(1)}, bf16[128,1024]{1,0:T(8,128)(2,1)}, u32[]{:S(2)}) copy-start(bf16[128,1024]{1,0:T(8,128)(2,1)} %get-tuple-element.27) | copy-start | bytes 786436
  124.5 2.9 %copy-start.4 = (bf16[128,1024]{1,0:T(8,128)(2,1)S(1)}, bf16[128,1024]{1,0:T(8,128)(2,1)}, u32[]{:S(2)}) copy-start(bf16[128,1024]{1,0:T(8,128)(2,1)} %get-tuple-element.50) | copy-start | bytes 786436

commit v2 on v1

--- a/solution.py
+++ b/solution.py
@@ -64,24 +64,32 @@
     )
 
 
-def kernel(
+def layer(
     order_ref,
     seg_ref,
-    x_ref,
-    g_ref,
-    vec_ref,
+    x_hbm,
+    g_hbm,
+    ln1g_ref,
+    ln1b_ref,
+    bout_ref,
+    ln2g_ref,
+    ln2b_ref,
+    bdown_ref,
+    bup_ref,
+    bqv_ref,
     wqkv_hbm,
     wout_hbm,
     wup_hbm,
     wdn_hbm,
     y_out,
     gin_out,
-    gup_out,
-    gdn_out,
-    gwo_out,
-    gqkv_out,
+    oa_out,
+    ob_out,
+    oc_out,
     vec_out,
     ctx_out,
+    x_ref,
+    g_ref,
     wqkv,
     wout,
     wup,
@@ -171,10 +179,149 @@
             device_id_type=MESH,
         )
 
+    sends = []
+    arrivals = {}
+
     def each(low, high, step):
         @pl.loop(low, high)
         def _(d):
             step(d)
+
+    loads = [
+        pltpu.make_async_copy(
+            wqkv_hbm.at[i], wqkv.at[:, pl.ds(128 * i, 128)], load_sem.at[i]
+        )
+        for i in range(3)
+    ] + [
+        pltpu.make_async_copy(wdn_hbm, wdn, load_sem.at[3]),
+        pltpu.make_async_copy(wout_hbm, wout, load_sem.at[4]),
+        pltpu.make_async_copy(wup_hbm, wup, load_sem.at[5]),
+        pltpu.make_async_copy(x_hbm, x_ref, load_sem.at[6]),
+        pltpu.make_async_copy(g_hbm, g_ref, load_sem.at[7]),
+    ]
+    for i in (6, 0, 1, 2, 7, 3, 4, 5):
+        loads[i].start()
+
+    def combine(buf, kept, index):
+        return pltpu.make_async_remote_copy(
+            src_ref=buf.at[pl.ds(pl.multiple_of(other * 8, 8), 8)],
+            dst_ref=kept,
+            send_sem=cs_s.at[index],
+            recv_sem=cs_r.at[index],
+            device_id={"ctx": partner},
+            device_id_type=MESH,
+        )
+
+    def combine_start(buf, kept, index):
+        combine(buf, kept, index).start()
+        sends.append(lambda: combine(buf, kept, index).wait_send())
+        arrivals[100 + index] = lambda: combined(buf, kept, index)
+
+    def combined(buf, kept, index):
+        arrivals.pop(100 + index)
+        combine(buf, kept, index).wait_recv()
+
+        @pl.loop(0, 8)
+        def _(j):
+            buf[core * 8 + j] = (buf[core * 8 + j].astype(F32) + kept[j].astype(F32)).astype(BF)
+
+    def scatter_start(buf, recv, kind):
+        sends.append(
+            lambda: each(
+                1, 8, lambda d: to_chip(buf.at[slot], buf.at[slot], kind, d).wait_send()
+            )
+        )
+        arrivals[kind] = lambda: scatter_end(buf, recv, kind)
+        each(
+            1,
+            8,
+            lambda d: to_chip(
+                buf.at[core * 8 + lax.rem(chip + d, 8)], recv.at[d], kind, d
+            ).start(),
+        )
+
+    def scatter_end(buf, recv, kind):
+        arrivals.pop(kind)
+        each(
+            1,
+            8,
+            lambda d: to_chip(
+                buf.at[core * 8 + lax.rem(chip + d, 8)], recv.at[d], kind, d
+            ).wait_recv(),
+        )
+        whole = buf[slot].astype(F32)
+        for d in range(1, 8):
+            whole = whole + recv[d].astype(F32)
+        return whole.astype(BF)
+
+    def spread_start(buf, kind, forward):
+        sends.append(lambda: spread_sent(buf, kind, forward))
+        arrivals[kind] = lambda: (
+            spread_pass(buf, kind, forward),
+            spread_end(buf, kind, forward),
+        )
+        to_partner(buf.at[slot], buf.at[slot], kind, 0).start()
+        each(1, 8, lambda d: to_chip(buf.at[slot], buf.at[slot], kind, d).start())
+
+    def spread_sent(buf, kind, forward):
+        to_partner(buf.at[slot], buf.at[slot], kind, 0).wait_send()
+
+        def sent(d):
+            to_chip(buf.at[slot], buf.at[slot], kind, d).wait_send()
+            to_partner(buf.at[slot], buf.at[slot], forward, d).wait_send()
+
+        each(1, 8, sent)
+
+    def spread_pass(buf, kind, forward):
+        arrivals[kind] = lambda: spread_end(buf, kind, forward)
+
+        def step(d):
+            s = core * 8 + lax.rem(chip + 8 - d, 8)
+            to_chip(buf.at[slot], buf.at[s], kind, d).wait_recv()
+            to_partner(buf.at[s], buf.at[s], forward, d).start()
+
+        each(1, 8, step)
+
+    def spread_end(buf, kind, forward):
+        arrivals.pop(kind)
+        s = other * 8 + chip
+        to_partner(buf.at[s], buf.at[s], kind, 0).wait_recv()
+
+        def step(d):
+            t = other * 8 + lax.rem(chip + 8 - d, 8)
+            to_partner(buf.at[t], buf.at[t], forward, d).wait_recv()
+
+        each(1, 8, step)
+
+    def reduce_start(part, send, recv, kind):
+        send[...] = part.astype(BF).reshape(8, 16, 1024)
+        each(1, 8, lambda d: to_wa(send.at[lax.rem(wa + d, 8)], recv.at[d], kind, d).start())
+        sends.append(lambda: wa_sent(send, kind))
+        arrivals[kind] = lambda: reduce_end(send, recv, kind)
+
+    def reduce_end(send, recv, kind):
+        arrivals.pop(kind)
+        each(1, 8, lambda d: to_wa(send.at[lax.rem(wa + d, 8)], recv.at[d], kind, d).wait_recv())
+        whole = send[wa].astype(F32)
+        for d in range(1, 8):
+            whole = whole + recv[d].astype(F32)
+        return whole
+
+    def gather_start(buf, kind):
+        each(1, 8, lambda d: to_wa(buf.at[wa], buf.at[wa], kind, d).start())
+        sends.append(lambda: wa_sent(buf, kind))
+        arrivals[kind] = lambda: gather_end(buf, kind)
+
+    def wa_sent(buf, kind):
+        each(1, 8, lambda d: to_wa(buf.at[wa], buf.at[wa], kind, d).wait_send())
+
+    def gather_end(buf, kind):
+        arrivals.pop(kind)
+        each(
+            1,
+            8,
+            lambda d: to_wa(buf.at[wa], buf.at[lax.rem(wa + 8 - d, 8)], kind, d).wait_recv(),
+        )
 
     barrier = pltpu.get_barrier_semaphore()
     each(
@@ -192,29 +339,22 @@
         ),
     )
 
-    loads = [
-        pltpu.make_async_copy(
-            wqkv_hbm.at[i], wqkv.at[:, pl.ds(128 * i, 128)], load_sem.at[i]
-        )
-        for i in range(3)
-    ] + [
-        pltpu.make_async_copy(wdn_hbm, wdn, load_sem.at[3]),
-        pltpu.make_async_copy(wout_hbm, wout, load_sem.at[4]),
-        pltpu.make_async_copy(wup_hbm, wup, load_sem.at[5]),
-    ]
-    for load in loads:
-        load.start()
-
-    ln1_gain = vec_ref[0:1, :]
-    ln1_bias = vec_ref[1:2, :]
-    b_out = vec_ref[2:3, :]
-    ln2_gain = vec_ref[3:4, :]
-    ln2_bias = vec_ref[4:5, :]
-    b_down = vec_ref[5:6, :]
-    b_up = vec_ref[6:7, 0:512]
-    b_q = vec_ref[7:8, 0:128]
-    b_v = vec_ref[7:8, 128:256]
-
+    def vector(ref):
+        rows = ref[...].astype(F32)
+        return jnp.concatenate([rows[j : j + 1, :] for j in range(rows.shape[0])], axis=1)
+
+    ln1_gain = vector(ln1g_ref)
+    ln1_bias = vector(ln1b_ref)
+    b_out = vector(bout_ref)
+    ln2_gain = vector(ln2g_ref)
+    ln2_bias = vector(ln2b_ref)
+    b_down = vector(bdown_ref)
+    b_up = vector(bup_ref)
+    b_qv = bqv_ref[...].astype(F32)
+    b_q = b_qv[0:1, :]
+    b_v = b_qv[1:2, :]
+
+    loads[6].wait()
     xhat, _ = normalize(x_ref[...].astype(F32))
     xhat_all[...] = xhat
     normed[...] = (xhat * ln1_gain + ln1_bias).astype(BF)
@@ -227,6 +367,8 @@
 
     to_partner(kv.at[slot], kv.at[slot], KV, 0).start()
     each(1, 8, lambda d: to_chip(kv.at[slot], kv.at[slot], KV, d).start())
+    sends.append(lambda: spread_sent(kv, KV, KVF))
+    arrivals[KV] = lambda: (spread_pass(kv, KV, KVF), spread_end(kv, KV, KVF))
 
     q_low = (proj[:, 0:128] + b_q).astype(BF) * jnp.asarray(0.125, BF)
     lane = lax.broadcasted_iota(jnp.int32, (128, 128), 1)
@@ -268,6 +410,7 @@
         scores[s] = masked
         return jnp.maximum(top, jnp.max(masked.reshape(16, 8, 256), axis=0))
 
+    loads[7].wait()
     loads[3].wait()
     dm[...] = nt(g_ref[...], wdn[...])
 
@@ -289,6 +432,7 @@
         return score(s, top)
 
     top = lax.fori_loop(1, 8, far, top)
+    arrivals.pop(KV)
 
     top = jnp.max(top, axis=0, keepdims=True)
     acc[...] = jnp.zeros_like(acc)
@@ -309,27 +453,6 @@
     raw_t = diagonal(acc[...] / total)
     attn_t[...] = raw_t
     attn_low[...] = raw_t.T.astype(BF)
-
-    def reduce_start(part, send, recv, kind):
-        send[...] = part.astype(BF).reshape(8, 16, 1024)
-        each(1, 8, lambda d: to_wa(send.at[lax.rem(wa + d, 8)], recv.at[d], kind, d).start())
-
-    def reduce_end(send, recv, kind):
-        each(1, 8, lambda d: to_wa(send.at[lax.rem(wa + d, 8)], recv.at[d], kind, d).wait_recv())
-        whole = send[wa].astype(F32)
-        for d in range(1, 8):
-            whole = whole + recv[d].astype(F32)
-        return whole
-
-    def gather_start(buf, kind):
-        each(1, 8, lambda d: to_wa(buf.at[wa], buf.at[wa], kind, d).start())
-
-    def gather_end(buf, kind):
-        each(
-            1,
-            8,
-            lambda d: to_wa(buf.at[wa], buf.at[lax.rem(wa + 8 - d, 8)], kind, d).wait_recv(),
-        )
 
     loads[4].wait()
     reduce_start(nn(attn_low[...], wout[...]), rs1s, rs1r, RS1)
@@ -358,68 +481,7 @@
     ga[:, 64:96, :] = down[:, 0:512].reshape(16, 32, 512)
     ga[:, 96:128, :] = down[:, 512:1024].reshape(16, 32, 512)
 
-    def combine(buf, kept, index):
-        return pltpu.make_async_remote_copy(
-            src_ref=buf.at[pl.ds(pl.multiple_of(other * 8, 8), 8)],
-            dst_ref=kept,
-            send_sem=cs_s.at[index],
-            recv_sem=cs_r.at[index],
-            device_id={"ctx": partner},
-            device_id_type=MESH,
-        )
-
-    def combined(buf, kept, index):
-        combine(buf, kept, index).wait_recv()
-
-        @pl.loop(0, 8)
-        def _(j):
-            buf[core * 8 + j] = (buf[core * 8 + j].astype(F32) + kept[j].astype(F32)).astype(BF)
-
-    def scatter_start(buf, recv, kind):
-        each(
-            1,
-            8,
-            lambda d: to_chip(
-                buf.at[core * 8 + lax.rem(chip + d, 8)], recv.at[d], kind, d
-            ).start(),
-        )
-
-    def scatter_end(buf, recv, kind):
-        each(
-            1,
-            8,
-            lambda d: to_chip(
-                buf.at[core * 8 + lax.rem(chip + d, 8)], recv.at[d], kind, d
-            ).wait_recv(),
-        )
-        whole = buf[slot].astype(F32)
-        for d in range(1, 8):
-            whole = whole + recv[d].astype(F32)
-        return whole.astype(BF)
-
-    def spread_start(buf, kind):
-        to_partner(buf.at[slot], buf.at[slot], kind, 0).start()
-        each(1, 8, lambda d: to_chip(buf.at[slot], buf.at[slot], kind, d).start())
-
-    def spread_pass(buf, kind, forward):
-        def step(d):
-            s = core * 8 + lax.rem(chip + 8 - d, 8)
-            to_chip(buf.at[slot], buf.at[s], kind, d).wait_recv()
-            to_partner(buf.at[s], buf.at[s], forward, d).start()
-
-        each(1, 8, step)
-
-    def spread_end(buf, kind, forward):
-        s = other * 8 + chip
-        to_partner(buf.at[s], buf.at[s], kind, 0).wait_recv()
-
-        def step(d):
-            t = other * 8 + lax.rem(chip + 8 - d, 8)
-            to_partner(buf.at[t], buf.at[t], forward, d).wait_recv()
-
-        each(1, 8, step)
-
-    combine(ga, pa, 0).start()
+    combine_start(ga, pa, 0)
 
     def vec_row(r, value):
         for j in range(8):
@@ -469,7 +531,7 @@
         dkv[s, :, 128:256] = nn(p.astype(BF), do2).astype(BF)
 
     each(0, 8, lambda j: back(other * 8 + j))
-    combine(dkv, pkv, 1).start()
+    combine_start(dkv, pkv, 1)
     each(0, 8, lambda j: back(core * 8 + j))
     combined(dkv, pkv, 1)
     scatter_start(dkv, rkv, RKV)
@@ -479,10 +541,10 @@
     d_out = tn(attn_low[...], dh_low).astype(BF)
     for s in range(16):
         gb[s, 0:64, :] = d_out[64 * (s % 2) : 64 * (s % 2) + 64, 128 * (s // 2) : 128 * (s // 2) + 128]
-    combine(gb, pb, 2).start()
+    combine_start(gb, pb, 2)
 
     oa[slot] = scatter_end(ga, ra, RA)
-    spread_start(oa, AGA)
+    spread_start(oa, AGA, FWA)
     combined(gb, pb, 2)
     scatter_start(gb, rb, RB)
 
@@ -493,12 +555,13 @@
     both = tn(normed[...], dkv_mine).astype(BF)
     gc[:, 0:64, :] = both[:, 0:128].reshape(16, 64, 128)
     gc[:, 64:128, :] = both[:, 128:256].reshape(16, 64, 128)
-    combine(gc, pc, 3).start()
+    combine_start(gc, pc, 3)
     vec_row(4, rows_sum(da * xhat_all[...]))
     vec_row(5, rows_sum(da))
     for j in range(8):
         vs[j, 6:8, :] = jnp.zeros((2, 128), F32)
     each(1, 8, lambda d: to_wa(vs.at[lax.rem(wa + d, 8)], vr.at[d], RS5, d).start())
+    sends.append(lambda: wa_sent(vs, RS5))
     cvs[12:13, :] = rows_sum(dq.astype(F32))
     cvs[13:14, :] = rows_sum(dkv_mine[:, 128:256].astype(F32))
     cvs[14:16, :] = jnp.zeros((2, 128), F32)
@@ -529,10 +592,11 @@
         )
 
     each(1, 16, lambda d: to_ctx(ctx, d).start())
+    sends.append(lambda: each(1, 16, lambda d: to_ctx(ctx, d).wait_send()))
     ob[slot] = scatter_end(gb, rb, RB)
-    spread_start(ob, AGB)
+    spread_start(ob, AGB, FWB)
     oc[slot] = scatter_end(gc, rc, RC)
-    spread_start(oc, AGCC)
+    spread_start(oc, AGCC, FWC)
     each(1, 16, lambda d: to_ctx(lax.rem(ctx + 16 - d, 16), d).wait_recv())
     ctx_sum = cvr[0]
     for i in range(1, 16):
@@ -544,61 +608,87 @@
     spread_pass(oc, AGCC, FWC)
 
     spread_end(oa, AGA, FWA)
-    gup_out[...] = oa[:, 0:64, :].reshape(1024, 512)
-    gdn_out[:, 0:512] = oa[:, 64:96, :].reshape(512, 512)
-    gdn_out[:, 512:1024] = oa[:, 96:128, :].reshape(512, 512)
+    oa_out[...] = oa[...]
     gather_end(y_all, AGY)
     y_out[...] = y_all[...].reshape(128, 1024)
     gather_end(g_all, AGG)
     gin_out[...] = g_all[...].reshape(128, 1024)
     spread_end(ob, AGB, FWB)
-    for s in range(16):
-        gwo_out[64 * (s % 2) : 64 * (s % 2) + 64, 128 * (s // 2) : 128 * (s // 2) + 128] = ob[
-            s, 0:64, :
-        ]
-    gqkv_out[0] = ob[:, 64:128, :].reshape(1024, 128)
+    ob_out[...] = ob[...]
     spread_end(oc, AGCC, FWC)
-    gqkv_out[1] = oc[:, 0:64, :].reshape(1024, 128)
-    gqkv_out[2] = oc[:, 64:128, :].reshape(1024, 128)
+    oc_out[...] = oc[...]
     gather_end(vall, AGV)
     vec_out[...] = vall[...]
 
-    for buf, kind, forward in ((kv, KV, KVF), (oa, AGA, FWA), (ob, AGB, FWB), (oc, AGCC, FWC)):
-        to_partner(buf.at[slot], buf.at[slot], kind, 0).wait_send()
-
-        def sent(d, buf=buf, kind=kind, forward=forward):
-            to_chip(buf.at[slot], buf.at[slot], kind, d).wait_send()
-            to_partner(buf.at[slot], buf.at[slot], forward, d).wait_send()
-
-        each(1, 8, sent)
-    for buf, kind in (
-        (rs1s, RS1),
-        (rs2s, RS2),
-        (rs3s, RS3),
-        (rs4s, RS4),
-        (c_all, AGC),
-        (dh_all, AGD),
-        (y_all, AGY),
-        (g_all, AGG),
-        (vs, RS5),
-        (vall, AGV),
-    ):
-        each(
-            1,
-            8,
-            lambda d, buf=buf, kind=kind: to_wa(buf.at[wa], buf.at[wa], kind, d).wait_send(),
-        )
-    for buf, kind in ((ga, RA), (dkv, RKV), (gb, RB), (gc, RC)):
-        each(
-            1,
-            8,
-            lambda d, buf=buf, kind=kind: to_chip(
-                buf.at[slot], buf.at[slot], kind, d
-            ).wait_send(),
-        )
-    for index, (buf, kept) in enumerate(((ga, pa), (dkv, pkv), (gb, pb), (gc, pc))):
-        combine(buf, kept, index).wait_send()
-    each(1, 16, lambda d: to_ctx(ctx, d).wait_send())
+    for sent in sends:
+        sent()
+
+
+def finish(
+    y_ref,
+    gin_ref,
+    oa_ref,
+    ob_ref,
+    oc_ref,
+    vec_ref,
+    ctx_ref,
+    y_out,
+    gin_out,
+    ln1g_out,
+    ln1b_out,
+    gqkv_out,
+    bqv_out,
+    gwo_out,
+    bout_out,
+    ln2g_out,
+    ln2b_out,
+    gup_out,
+    bup_out,
+    gdn_out,
+    bdown_out,
+    gin,
+    gqkv,
+    gwo,
+    gup,
+    gdn,
+    sems,
+):
+    copies = []
+
+    def leave(src, dst):
+        copies.append(pltpu.make_async_copy(src, dst, sems.at[len(copies)]))
+        copies[-1].start()
+
+    leave(y_ref, y_out)
+    for i in range(4):
+        rows = pl.ds(256 * i, 256)
+        gup[rows, :] = oa_ref[4 * i : 4 * i + 4, 0:64, :].astype(F32).reshape(256, 512)
+        leave(gup.at[rows], gup_out.at[rows])
+    for i in range(4):
+        rows = pl.ds(128 * i, 128)
+        part = oa_ref[4 * i : 4 * i + 4, 64:128, :].astype(F32)
+        gdn[rows, 0:512] = part[:, 0:32].reshape(128, 512)
+        gdn[rows, 512:1024] = part[:, 32:64].reshape(128, 512)
+        leave(gdn.at[rows], gdn_out.at[rows])
+    gin[...] = gin_ref[...].astype(F32)
+    leave(gin, gin_out)
+    for s in range(16):
+        gwo[64 * (s % 2) : 64 * (s % 2) + 64, 128 * (s // 2) : 128 * (s // 2) + 128] = ob_ref[
+            s, 0:64, :
+        ].astype(F32)
+    leave(gwo, gwo_out)
+    gqkv[0] = ob_ref[:, 64:128, :].astype(F32).reshape(1024, 128)
+    leave(gqkv.at[0], gqkv_out.at[0])
+    gqkv[1] = oc_ref[:, 0:64, :].astype(F32).reshape(1024, 128)
+    leave(gqkv.at[1], gqkv_out.at[1])
+    gqkv[2] = oc_ref[:, 64:128, :].astype(F32).reshape(1024, 128)
+    leave(gqkv.at[2], gqkv_out.at[2])
+    for r, out in enumerate((ln2g_out, ln2b_out, bout_out, bdown_out, ln1g_out, ln1b_out)):
+        out[...] = vec_ref[:, r, :]
+    bup_out[...] = ctx_ref[0:4, :]
+    bqv_out[...] = ctx_ref[4:6, :]
+    for copy in copies:
+        copy.wait()
 
 
 def body(
@@ -619,21 +709,13 @@
     w_down,
     b_down,
 ):
-    vectors = jnp.stack(
-        [
-            ln1_gain,
-            ln1_bias,
-            b_out,
-            ln2_gain,
-            ln2_bias,
-            b_down,
-            jnp.pad(b_up, (0, 512)),
-            jnp.pad(b_qv.reshape(256), (0, 768)),
-        ]
-    ).astype(F32)
     vmem = pl.BlockSpec(memory_space=pltpu.VMEM)
     smem = pl.BlockSpec(memory_space=pltpu.SMEM)
     hbm = pl.BlockSpec(memory_space=pl.ANY)
+    far = pl.BlockSpec(memory_space=pltpu.HBM)
+
+    def stay(operand):
+        return pltpu.with_memory_space_constraint(operand, pltpu.HBM)
 
     def bf(*shape):
         return pltpu.VMEM(shape, BF)
@@ -642,25 +724,26 @@
         return pltpu.VMEM(shape, F32)
 
     outs = pl.pallas_call(
-        kernel,
+        layer,
         out_shape=(
             jax.ShapeDtypeStruct((128, 1024), BF),
             jax.ShapeDtypeStruct((128, 1024), BF),
-            jax.ShapeDtypeStruct((1024, 512), BF),
-            jax.ShapeDtypeStruct((512, 1024), BF),
-            jax.ShapeDtypeStruct((128, 1024), BF),
-            jax.ShapeDtypeStruct((3, 1024, 128), BF),
+            jax.ShapeDtypeStruct((16, 128, 512), BF),
+            jax.ShapeDtypeStruct((16, 128, 128), BF),
+            jax.ShapeDtypeStruct((16, 128, 128), BF),
             jax.ShapeDtypeStruct((8, 8, 128), F32),
             jax.ShapeDtypeStruct((8, 128), F32),
         ),
-        in_specs=[smem, vmem, vmem, vmem, vmem, hbm, hbm, hbm, hbm],
-        out_specs=(vmem,) * 8,
+        in_specs=[smem, vmem, far, far] + [vmem] * 8 + [far] * 4,
+        out_specs=(vmem,) * 7,
         scratch_shapes=[
+            bf(128, 1024),
+            bf(128, 1024),
             bf(1024, 384),
             bf(128, 1024),
             bf(1024, 512),
             bf(512, 1024),
-            pltpu.SemaphoreType.DMA((6,)),
+            pltpu.SemaphoreType.DMA((8,)),
             f32(128, 1024),
             bf(128, 1024),
             bf(16, 128, 256),
@@ -708,41 +791,60 @@
             pltpu.SemaphoreType.DMA((20,)),
         ],
         compiler_params=pltpu.CompilerParams(
-            collective_id=0, has_side_effects=True, vmem_limit_bytes=56 << 20
+            collective_id=0, has_side_effects=True, vmem_limit_bytes=32 << 20
         ),
-        name="layer",
+        name="decoder",
     )(
         block_order,
         seg_ids.reshape(16, 128),
-        layer_input,
-        cotangent,
-        vectors,
-        w_qkv.transpose(1, 0, 2),
-        w_out,
-        w_up,
-        w_down,
-    )
-    y, gin, gup, gdn, gwo, gqkv, vec, ctx_vec = outs
-
-    def whole(r):
-        return vec[:, r, :].reshape(1024)
-
-    return (
-        y,
-        gin.astype(F32),
-        whole(4),
-        whole(5),
-        gqkv.astype(F32).transpose(1, 0, 2),
-        ctx_vec[4:6, :],
-        gwo.astype(F32),
-        whole(2),
-        whole(0),
-        whole(1),
-        gup.astype(F32),
-        ctx_vec[0:4, :].reshape(512),
-        gdn.astype(F32),
-        whole(3),
-    )
+        stay(layer_input),
+        stay(cotangent),
+        *(v.reshape(-1, 128) for v in (ln1_gain, ln1_bias, b_out, ln2_gain, ln2_bias, b_down, b_up)),
+        b_qv,
+        stay(w_qkv.transpose(1, 0, 2)),
+        stay(w_out),
+        stay(w_up),
+        stay(w_down),
+    )
+    shapes = (
+        ((128, 1024), BF),
+        ((128, 1024), F32),
+        ((8, 128), F32),
+        ((8, 128), F32),
+        ((3, 1024, 128), F32),
+        ((2, 128), F32),
+        ((128, 1024), F32),
+        ((8, 128), F32),
+        ((8, 128), F32),
+        ((8, 128), F32),
+        ((1024, 512), F32),
+        ((4, 128), F32),
+        ((512, 1024), F32),
+        ((8, 128), F32),
+    )
+    large = (0, 1, 4, 6, 10, 12)
+    done = list(
+        pl.pallas_call(
+            finish,
+            out_shape=tuple(jax.ShapeDtypeStruct(*shape) for shape in shapes),
+            in_specs=[vmem] * 7,
+            out_specs=tuple(hbm if i in large else vmem for i in range(14)),
+            scratch_shapes=[
+                f32(128, 1024),
+                f32(3, 1024, 128),
+                f32(128, 1024),
+                f32(1024, 512),
+                f32(512, 1024),
+                pltpu.SemaphoreType.DMA((14,)),
+            ],
+            compiler_params=pltpu.CompilerParams(vmem_limit_bytes=24 << 20),
+            name="finish",
+        )(*outs)
+    )
+    for i in (2, 3, 7, 8, 9, 11, 13):
+        done[i] = done[i].reshape(-1)
+    done[4] = done[4].transpose(1, 0, 2)
+    return tuple(done)
 
 
 def solution(mesh):

time: 129 us -> 118 us (0.915)
  other arithmetic: 7.95 us -> 0 us
  local copies, waits for them, and re-layouts: 10.5 us -> 6.76 us
    convert_element_type x5 -> x0, other arithmetic: 6.71 us -> none  [the longest x1 2.83 us: body(): gup.astype(F32)]
    unnamed x11 -> x20, local copies, waits for them, and re-layouts: 0.72 us -> 6.76 us
    another operation x9 -> x0, local copies, waits for them, and re-layouts: 4.19 us -> none  [body(): jnp.stack([ln1_gain, ln1_bias, b_out, ln2_gain, ln2_bias, b_down, jnp.pad...]
    slice x2 -> x0, local copies, waits for them, and re-layouts: 2.95 us -> none  [the longest x1 1.71 us: whole(): return vec[:, r, :].reshape(1024)]
    pad x2 -> x0, local copies, waits for them, and re-layouts: 1.34 us -> none  [the longest x1 0.69 us: body(): jnp.pad(b_up, (0, 512))]
    pallas_call x1 -> x2, Pallas kernels: 109 us -> 110 us  [the longest x1 107 us: body(): pl.pallas_call(layer, out_shape=(jax.ShapeDtypeStruct((128, 1024), BF), j...]
where the time goes in v2:
time: 118 us
  Pallas kernels  110 us (93%)
  local copies, waits for them, and re-layouts  6.76 us (6%)
    pallas_call x1, Pallas kernels, body(): pl.pallas_call(layer, out_shape=(jax.ShapeDtypeStruct((128, 1024), BF), j...  107 us
    unnamed x20, local copies, waits for them, and re-layouts  6.76 us
    pallas_call x1, Pallas kernels, body(): pl.pallas_call(finish, out_shape=tuple((jax.ShapeDtypeStruct(*shape) for...  3.64 us

profile of v2, /device:TPU:1, one launch (start us, length us, event | category | flops | bytes accessed | tf_op | source)
XLA Modules:
  0.0 117.8 jit_solution(2859622884838194803)
XLA Ops:
  0.7 0.0 copy-start
  0.7 0.7 copy-done
  1.4 0.0 copy-start.1
  1.4 0.7 copy-done.1
  2.0 0.0 copy-start.2
  2.0 0.7 copy-done.2
  2.7 0.0 copy-start.3
  2.7 0.7 copy-done.3
  3.4 0.0 copy-start.4
  3.4 0.7 copy-done.4
  4.1 0.0 copy-start.5
  4.1 0.7 copy-done.5
  4.8 0.0 copy-start.6
  4.8 0.7 copy-done.6
  5.4 0.0 copy-start.7
  5.4 0.7 copy-done.7
  6.1 0.0 copy-start.8
  6.1 0.7 copy-done.8
  6.8 0.0 copy-start.9
  6.8 0.7 copy-done.9
  7.4 106.7 %decoder.1 = (bf16[128,1024]{1,0:T(8,128)(2,1)S(1)}, bf16[128,1024]{1,0:T(8,128)(2,1)S(1)}, bf16[16,128,512]{2,1,0:T(8,128)(2,1)S(1)}, bf16[16,128,128]{2,1,0:T(...) custom-call(s32[32]{0:T(128)S(1)} %copy-done.8, ...), custom_call_target="tpu_custom_call" | custom-call | tf_op jit(solution)/shard_map/decoder/pallas_call | solution.py:726
  114.2 3.6 %finish.1 = (bf16[128,1024]{1,0:T(8,128)(2,1)}, f32[128,1024]{1,0:T(8,128)}, f32[8,128]{1,0:T(8,128)}, f32[8,128]{1,0:T(8,128)}, f32[3,1024,128]{2,1,0:T(8,128)}...) custom-call(bf16[128,1024]{1,0:T(8,128)(2,1)S(1)} %get-tuple-element, ...), custom_call_target="tpu_custom_call" | custom-call | tf_op jit(solution)/shard_map/finish/pallas_call | solution.py:827
Async XLA Ops:
  0.7 0.7 copy-start
  1.4 0.7 copy-start.1
  2.0 0.7 copy-start.2
  2.7 0.7 copy-start.3
  3.4 0.7 copy-start.4
  4.1 0.7 copy-start.5
  4.8 0.7 copy-start.6
  5.4 0.7 copy-start.7
  6.1 0.7 copy-start.8
  6.8 0.7 copy-start.9

commit v3 on v2

--- a/solution.py
+++ b/solution.py
@@ -12,19 +12,23 @@
 GELU_B = 0.044715
 
 (
-    KV,
-    KVF,
+    KK,
+    KKF,
+    VV,
+    VVF,
     RS1,
     AGC,
     RS2,
     RS3,
     AGD,
     AGY,
-    CMB,
     RKV,
-    RA,
-    AGA,
-    FWA,
+    RU,
+    AGU,
+    FWU,
+    RD,
+    AGW,
+    FWW,
     RB,
     AGB,
     FWB,
@@ -36,7 +40,7 @@
     AGG,
     AGV,
     NSEM,
-) = range(24)
+) = range(28)
 
 
 def nn(a, b):
@@ -65,10 +69,34 @@
 
 
 def layer(
+    order_hbm,
+    seg_hbm,
+    x_hbm,
+    g_hbm,
+    ln1g_hbm,
+    ln1b_hbm,
+    bout_hbm,
+    ln2g_hbm,
+    ln2b_hbm,
+    bdown_hbm,
+    bup_hbm,
+    bqv_hbm,
+    wqkv_hbm,
+    wout_hbm,
+    wup_hbm,
+    wdn_hbm,
+    y_out,
+    gin_out,
+    ou_out,
+    od_out,
+    ob_out,
+    oc_out,
+    vec_out,
+    ctx_out,
     order_ref,
     seg_ref,
-    x_hbm,
-    g_hbm,
+    x_ref,
+    g_ref,
     ln1g_ref,
     ln1b_ref,
     bout_ref,
@@ -77,19 +105,6 @@
     bdown_ref,
     bup_ref,
     bqv_ref,
-    wqkv_hbm,
-    wout_hbm,
-    wup_hbm,
-    wdn_hbm,
-    y_out,
-    gin_out,
-    oa_out,
-    ob_out,
-    oc_out,
-    vec_out,
-    ctx_out,
-    x_ref,
-    g_ref,
     wqkv,
     wout,
     wup,
@@ -97,7 +112,8 @@
     load_sem,
     xhat_all,
     normed,
-    kv,
+    k_all,
+    v_all,
     q2,
     scores,
     acc,
@@ -116,10 +132,14 @@
     dkv,
     pkv,
     rkv,
-    ga,
-    pa,
-    ra,
-    oa,
+    gu,
+    pu,
+    ru,
+    ou,
+    gd,
+    pd,
+    rd,
+    od,
     gb,
     pb,
     rb,
@@ -199,7 +219,27 @@
         pltpu.make_async_copy(x_hbm, x_ref, load_sem.at[6]),
         pltpu.make_async_copy(g_hbm, g_ref, load_sem.at[7]),
     ]
-    for i in (6, 0, 1, 2, 7, 3, 4, 5):
+    small = [
+        pltpu.make_async_copy(src, dst, load_sem.at[8 + i])
+        for i, (src, dst) in enumerate(
+            (
+                (ln1g_hbm, ln1g_ref),
+                (ln1b_hbm, ln1b_ref),
+                (bqv_hbm, bqv_ref),
+                (order_hbm, order_ref),
+                (seg_hbm, seg_ref),
+                (bout_hbm, bout_ref),
+                (ln2g_hbm, ln2g_ref),
+                (ln2b_hbm, ln2b_ref),
+                (bdown_hbm, bdown_ref),
+                (bup_hbm, bup_ref),
+            )
+        )
+    ]
+    loads[6].start()
+    for load in small:
+        load.start()
+    for i in (1, 2, 0, 7, 3, 4, 5):
         loads[i].start()
 
     def combine(buf, kept, index):
@@ -343,34 +383,27 @@
         rows = ref[...].astype(F32)
         return jnp.concatenate([rows[j : j + 1, :] for j in range(rows.shape[0])], axis=1)
 
-    ln1_gain = vector(ln1g_ref)
-    ln1_bias = vector(ln1b_ref)
-    b_out = vector(bout_ref)
-    ln2_gain = vector(ln2g_ref)
-    ln2_bias = vector(ln2b_ref)
-    b_down = vector(bdown_ref)
-    b_up = vector(bup_ref)
-    b_qv = bqv_ref[...].astype(F32)
-    b_q = b_qv[0:1, :]
-    b_v = b_qv[1:2, :]
-
     loads[6].wait()
     xhat, _ = normalize(x_ref[...].astype(F32))
     xhat_all[...] = xhat
+    for load in small:
+        load.wait()
+    ln1_gain = vector(ln1g_ref)
+    ln1_bias = vector(ln1b_ref)
+    b_qv = bqv_ref[...].astype(F32)
     normed[...] = (xhat * ln1_gain + ln1_bias).astype(BF)
-    for i in range(3):
+    for i in range(1, 3):
         loads[i].wait()
-    proj = nn(normed[...], wqkv[...])
-    kv[slot, :, 0:128] = proj[:, 128:256].astype(BF)
-    kv[slot, :, 128:256] = (proj[:, 256:384] + b_v).astype(BF)
+    proj = nn(normed[...], wqkv[:, 128:384])
+    k_all[slot] = proj[:, 0:128].astype(BF)
+    v_all[slot] = (proj[:, 128:256] + b_qv[1:2, :]).astype(BF)
     pl.semaphore_wait(barrier, 22)
 
-    to_partner(kv.at[slot], kv.at[slot], KV, 0).start()
-    each(1, 8, lambda d: to_chip(kv.at[slot], kv.at[slot], KV, d).start())
-    sends.append(lambda: spread_sent(kv, KV, KVF))
-    arrivals[KV] = lambda: (spread_pass(kv, KV, KVF), spread_end(kv, KV, KVF))
-
-    q_low = (proj[:, 0:128] + b_q).astype(BF) * jnp.asarray(0.125, BF)
+    spread_start(k_all, KK, KKF)
+    spread_start(v_all, VV, VVF)
+
+    loads[0].wait()
+    q_low = (nn(normed[...], wqkv[:, 0:128]) + b_qv[0:1, :]).astype(BF) * jnp.asarray(0.125, BF)
     lane = lax.broadcasted_iota(jnp.int32, (128, 128), 1)
     zero = jnp.zeros((128, 128), BF)
     q2[0:128, :] = jnp.where(lane < 64, q_low, zero)
@@ -400,7 +433,7 @@
     row = lax.broadcasted_iota(jnp.int32, (128, 256), 0)
 
     def score(s, top):
-        keys = kv[s, :, 0:128]
+        keys = k_all[s]
         owner = 2 * lax.rem(s, 8) + lax.div(s, 8)
         k_pos = jnp.where(
             row < 64, row + 64 * order_ref[2 * owner], row - 64 + 64 * order_ref[2 * owner + 1]
@@ -410,36 +443,41 @@
         scores[s] = masked
         return jnp.maximum(top, jnp.max(masked.reshape(16, 8, 256), axis=0))
 
+    top = score(slot, jnp.full((8, 256), -1e30, F32))
     loads[7].wait()
     loads[3].wait()
     dm[...] = nt(g_ref[...], wdn[...])
-
-    top = score(slot, jnp.full((8, 256), -1e30, F32))
-    to_partner(kv.at[slot], kv.at[slot], KV, 0).wait_recv()
-    top = score(other * 8 + chip, top)
+    b_out = vector(bout_ref)
+    ln2_gain = vector(ln2g_ref)
+    ln2_bias = vector(ln2b_ref)
+    b_down = vector(bdown_ref)
+    b_up = vector(bup_ref)
 
     def near(d, top):
         s = core * 8 + lax.rem(chip + 8 - d, 8)
-        to_chip(kv.at[slot], kv.at[s], KV, d).wait_recv()
-        to_partner(kv.at[s], kv.at[s], KVF, d).start()
+        to_chip(k_all.at[slot], k_all.at[s], KK, d).wait_recv()
+        to_partner(k_all.at[s], k_all.at[s], KKF, d).start()
         return score(s, top)
 
     top = lax.fori_loop(1, 8, near, top)
+    to_partner(k_all.at[slot], k_all.at[other * 8 + chip], KK, 0).wait_recv()
+    top = score(other * 8 + chip, top)
+    spread_pass(v_all, VV, VVF)
 
     def far(d, top):
         s = other * 8 + lax.rem(chip + 8 - d, 8)
-        to_partner(kv.at[s], kv.at[s], KVF, d).wait_recv()
+        to_partner(k_all.at[s], k_all.at[s], KKF, d).wait_recv()
         return score(s, top)
 
     top = lax.fori_loop(1, 8, far, top)
-    arrivals.pop(KV)
-
+    arrivals.pop(KK)
+    spread_end(v_all, VV, VVF)
     top = jnp.max(top, axis=0, keepdims=True)
     acc[...] = jnp.zeros_like(acc)
 
     def mix(s, total):
         p = jnp.exp(scores[s] - top)
-        acc[...] += tn(kv[s, :, 128:256], p.astype(BF))
+        acc[...] += tn(v_all[s], p.astype(BF))
         return total + jnp.sum(p.reshape(16, 8, 256), axis=0)
 
     total = lax.fori_loop(0, 16, mix, jnp.zeros((8, 256), F32))
@@ -475,13 +513,12 @@
     du = (dm[...] * slope).astype(BF)
     act = (0.5 * up * (1.0 + tanh)).astype(BF)
     reduce_start(nt(du, wup[...]), rs2s, rs2r, RS2)
-    reduce_start(nn(act, wdn[...]), rs3s, rs3r, RS3)
-    ga[:, 0:64, :] = tn(c_low, du).astype(BF).reshape(16, 64, 512)
+    gu[...] = tn(c_low, du).astype(BF).reshape(16, 64, 512)
+    combine_start(gu, pu, 0)
     down = tn(act, g_ref[...]).astype(BF)
-    ga[:, 64:96, :] = down[:, 0:512].reshape(16, 32, 512)
-    ga[:, 96:128, :] = down[:, 512:1024].reshape(16, 32, 512)
-
-    combine_start(ga, pa, 0)
+    gd[:, 0:32, :] = down[:, 0:512].reshape(16, 32, 512)
+    gd[:, 32:64, :] = down[:, 512:1024].reshape(16, 32, 512)
+    combine_start(gd, pd, 1)
 
     def vec_row(r, value):
         for j in range(8):
@@ -498,14 +535,14 @@
     d_hidden = g_mine + norm_back(dc, ln2_gain, hat_two, rstd_two)
     dh_all[wa] = d_hidden.astype(BF)
     gather_start(dh_all, AGD)
-    combined(ga, pa, 0)
-    scatter_start(ga, ra, RA)
+    combined(gu, pu, 0)
+    scatter_start(gu, ru, RU)
+    combined(gd, pd, 1)
+    scatter_start(gd, rd, RD)
     vec_row(0, rows_sum(dc * hat_two))
     vec_row(1, rows_sum(dc))
     vec_row(2, rows_sum(d_hidden))
     vec_row(3, rows_sum(g_mine))
-    y_all[wa] = (hidden + reduce_end(rs3s, rs3r, RS3) + b_down).astype(BF)
-    gather_start(y_all, AGY)
     gather_end(dh_all, AGD)
 
     dh_low = dh_all[...].reshape(128, 1024)
@@ -525,15 +562,15 @@
 
     def back(s):
         p = jnp.exp(scores[s] - lse)
-        ds = (p * (nt(kv[s, :, 128:256], do2) - delta)).astype(BF)
-        acc[...] += tn(kv[s, :, 0:128], ds)
+        ds = (p * (nt(v_all[s], do2) - delta)).astype(BF)
+        acc[...] += tn(k_all[s], ds)
         dkv[s, :, 0:128] = nn(ds, q2[...]).astype(BF)
         dkv[s, :, 128:256] = nn(p.astype(BF), do2).astype(BF)
 
     each(0, 8, lambda j: back(other * 8 + j))
-    combine_start(dkv, pkv, 1)
+    combine_start(dkv, pkv, 2)
     each(0, 8, lambda j: back(core * 8 + j))
-    combined(dkv, pkv, 1)
+    combined(dkv, pkv, 2)
     scatter_start(dkv, rkv, RKV)
 
     dq = (diagonal(acc[...]) * 0.125).T.astype(BF)
@@ -541,21 +578,22 @@
     d_out = tn(attn_low[...], dh_low).astype(BF)
     for s in range(16):
         gb[s, 0:64, :] = d_out[64 * (s % 2) : 64 * (s % 2) + 64, 128 * (s // 2) : 128 * (s // 2) + 128]
-    combine_start(gb, pb, 2)
-
-    oa[slot] = scatter_end(ga, ra, RA)
-    spread_start(oa, AGA, FWA)
-    combined(gb, pb, 2)
-    scatter_start(gb, rb, RB)
+    combine_start(gb, pb, 3)
+    reduce_start(nn(act, wdn[...]), rs3s, rs3r, RS3)
+    ou[slot] = scatter_end(gu, ru, RU)
+    od[slot] = scatter_end(gd, rd, RD)
 
     dkv_mine = scatter_end(dkv, rkv, RKV)
     d_qkv = jnp.concatenate([dq, dkv_mine], axis=1)
     da = nt(d_qkv, wqkv[...])
     reduce_start(da, rs4s, rs4r, RS4)
+    spread_start(ou, AGU, FWU)
     both = tn(normed[...], dkv_mine).astype(BF)
     gc[:, 0:64, :] = both[:, 0:128].reshape(16, 64, 128)
     gc[:, 64:128, :] = both[:, 128:256].reshape(16, 64, 128)
-    combine_start(gc, pc, 3)
+    combine_start(gc, pc, 4)
+    combined(gb, pb, 3)
+    scatter_start(gb, rb, RB)
     vec_row(4, rows_sum(da * xhat_all[...]))
     vec_row(5, rows_sum(da))
     for j in range(8):
@@ -565,9 +603,9 @@
     cvs[12:13, :] = rows_sum(dq.astype(F32))
     cvs[13:14, :] = rows_sum(dkv_mine[:, 128:256].astype(F32))
     cvs[14:16, :] = jnp.zeros((2, 128), F32)
-    spread_pass(oa, AGA, FWA)
-    combined(gc, pc, 3)
+    combined(gc, pc, 4)
     scatter_start(gc, rc, RC)
+    spread_start(od, AGW, FWW)
 
     hat_one, rstd_one = normalize(x_mine)
     d_first = reduce_end(rs4s, rs4r, RS4)
@@ -585,14 +623,15 @@
         return pltpu.make_async_remote_copy(
             src_ref=cvs,
             dst_ref=cvr.at[dst],
-            send_sem=cs_s.at[4 + d],
-            recv_sem=cs_r.at[4 + d],
+            send_sem=cs_s.at[5 + d],
+            recv_sem=cs_r.at[5 + d],
             device_id={"ctx": lax.rem(ctx + d, 16)},
             device_id_type=MESH,
         )
 
     each(1, 16, lambda d: to_ctx(ctx, d).start())
     sends.append(lambda: each(1, 16, lambda d: to_ctx(ctx, d).wait_send()))
+    spread_pass(ou, AGU, FWU)
     ob[slot] = scatter_end(gb, rb, RB)
     spread_start(ob, AGB, FWB)
     oc[slot] = scatter_end(gc, rc, RC)
@@ -604,11 +643,16 @@
     ctx_out[...] = ctx_sum[8:16, :]
     vall[wa] = ctx_sum[0:8, :]
     gather_start(vall, AGV)
+    spread_pass(od, AGW, FWW)
+    y_all[wa] = (hidden + reduce_end(rs3s, rs3r, RS3) + b_down).astype(BF)
+    gather_start(y_all, AGY)
     spread_pass(ob, AGB, FWB)
     spread_pass(oc, AGCC, FWC)
 
-    spread_end(oa, AGA, FWA)
-    oa_out[...] = oa[...]
+    spread_end(ou, AGU, FWU)
+    ou_out[...] = ou[...]
+    spread_end(od, AGW, FWW)
+    od_out[...] = od[...]
     gather_end(y_all, AGY)
     y_out[...] = y_all[...].reshape(128, 1024)
     gather_end(g_all, AGG)
@@ -627,7 +671,8 @@
 def finish(
     y_ref,
     gin_ref,
-    oa_ref,
+    ou_ref,
+    od_ref,
     ob_ref,
     oc_ref,
     vec_ref,
@@ -662,11 +707,11 @@
     leave(y_ref, y_out)
     for i in range(4):
         rows = pl.ds(256 * i, 256)
-        gup[rows, :] = oa_ref[4 * i : 4 * i + 4, 0:64, :].astype(F32).reshape(256, 512)
+        gup[rows, :] = ou_ref[4 * i : 4 * i + 4].astype(F32).reshape(256, 512)
         leave(gup.at[rows], gup_out.at[rows])
     for i in range(4):
         rows = pl.ds(128 * i, 128)
-        part = oa_ref[4 * i : 4 * i + 4, 64:128, :].astype(F32)
+        part = od_ref[4 * i : 4 * i + 4].astype(F32)
         gdn[rows, 0:512] = part[:, 0:32].reshape(128, 512)
         gdn[rows, 512:1024] = part[:, 32:64].reshape(128, 512)
         leave(gdn.at[rows], gdn_out.at[rows])
@@ -710,7 +755,6 @@
     b_down,
 ):
     vmem = pl.BlockSpec(memory_space=pltpu.VMEM)
-    smem = pl.BlockSpec(memory_space=pltpu.SMEM)
     hbm = pl.BlockSpec(memory_space=pl.ANY)
     far = pl.BlockSpec(memory_space=pltpu.HBM)
 
@@ -728,25 +772,37 @@
         out_shape=(
             jax.ShapeDtypeStruct((128, 1024), BF),
             jax.ShapeDtypeStruct((128, 1024), BF),
-            jax.ShapeDtypeStruct((16, 128, 512), BF),
+            jax.ShapeDtypeStruct((16, 64, 512), BF),
+            jax.ShapeDtypeStruct((16, 64, 512), BF),
             jax.ShapeDtypeStruct((16, 128, 128), BF),
             jax.ShapeDtypeStruct((16, 128, 128), BF),
             jax.ShapeDtypeStruct((8, 8, 128), F32),
             jax.ShapeDtypeStruct((8, 128), F32),
         ),
-        in_specs=[smem, vmem, far, far] + [vmem] * 8 + [far] * 4,
-        out_specs=(vmem,) * 7,
+        in_specs=[far] * 16,
+        out_specs=(vmem,) * 8,
         scratch_shapes=[
+            pltpu.SMEM((32,), jnp.int32),
+            pltpu.VMEM((16, 128), jnp.int32),
             bf(128, 1024),
             bf(128, 1024),
+            bf(8, 128),
+            bf(8, 128),
+            bf(8, 128),
+            bf(8, 128),
+            bf(8, 128),
+            bf(8, 128),
+            bf(4, 128),
+            bf(2, 128),
             bf(1024, 384),
             bf(128, 1024),
             bf(1024, 512),
             bf(512, 1024),
-            pltpu.SemaphoreType.DMA((8,)),
+            pltpu.SemaphoreType.DMA((18,)),
             f32(128, 1024),
             bf(128, 1024),
-            bf(16, 128, 256),
+            bf(16, 128, 128),
+            bf(16, 128, 128),
             bf(256, 128),
             f32(16, 128, 256),
             f32(128, 256),
@@ -765,10 +821,14 @@
             bf(16, 128, 256),
             bf(8, 128, 256),
             bf(8, 128, 256),
-            bf(16, 128, 512),
-            bf(8, 128, 512),
-            bf(8, 128, 512),
-            bf(16, 128, 512),
+            bf(16, 64, 512),
+            bf(8, 64, 512),
+            bf(8, 64, 512),
+            bf(16, 64, 512),
+            bf(16, 64, 512),
+            bf(8, 64, 512),
+            bf(8, 64, 512),
+            bf(16, 64, 512),
             bf(16, 128, 128),
             bf(8, 128, 128),
             bf(8, 128, 128),
@@ -787,20 +847,23 @@
             f32(16, 16, 128),
             pltpu.SemaphoreType.DMA((NSEM, 8)),
             pltpu.SemaphoreType.DMA((NSEM, 8)),
-            pltpu.SemaphoreType.DMA((20,)),
-            pltpu.SemaphoreType.DMA((20,)),
+            pltpu.SemaphoreType.DMA((21,)),
+            pltpu.SemaphoreType.DMA((21,)),
         ],
         compiler_params=pltpu.CompilerParams(
             collective_id=0, has_side_effects=True, vmem_limit_bytes=32 << 20
         ),
         name="decoder",
     )(
-        block_order,
-        seg_ids.reshape(16, 128),
+        stay(block_order),
+        stay(seg_ids.reshape(16, 128)),
         stay(layer_input),
         stay(cotangent),
-        *(v.reshape(-1, 128) for v in (ln1_gain, ln1_bias, b_out, ln2_gain, ln2_bias, b_down, b_up)),
-        b_qv,
+        *(
+            stay(v.reshape(-1, 128))
+            for v in (ln1_gain, ln1_bias, b_out, ln2_gain, ln2_bias, b_down, b_up)
+        ),
+        stay(b_qv),
         stay(w_qkv.transpose(1, 0, 2)),
         stay(w_out),
         stay(w_up),
@@ -827,7 +890,7 @@
         pl.pallas_call(
             finish,
             out_shape=tuple(jax.ShapeDtypeStruct(*shape) for shape in shapes),
-            in_specs=[vmem] * 7,
+            in_specs=[vmem] * 8,
             out_specs=tuple(hbm if i in large else vmem for i in range(14)),
             scratch_shapes=[
                 f32(128, 1024),

time: 118 us -> 114 us (0.966)
  local copies, waits for them, and re-layouts: 6.76 us -> 0 us
  Pallas kernels: 110 us -> 113 us
    unnamed x20 -> x0, local copies, waits for them, and re-layouts: 6.76 us -> none
    pallas_call x1, Pallas kernels: 107 us -> 110 us  [body(): pl.pallas_call(layer, out_shape=(jax.ShapeDtypeStruct((128, 1024), BF), j...]
where the time goes in v3:
time: 114 us
  Pallas kernels  113 us (99%)
    pallas_call x1, Pallas kernels, body(): pl.pallas_call(layer, out_shape=(jax.ShapeDtypeStruct((128, 1024), BF), j...  110 us
    pallas_call x1, Pallas kernels, body(): pl.pallas_call(finish, out_shape=tuple((jax.ShapeDtypeStruct(*shape) for...  3.64 us

profile of v3, /device:TPU:1, one launch (start us, length us, event | category | flops | bytes accessed | tf_op | source)
XLA Modules:
  0.0 113.9 jit_solution(731822165995920236)
XLA Ops:
  0.7 109.6 %decoder.1 = (bf16[128,1024]{1,0:T(8,128)(2,1)S(1)}, bf16[128,1024]{1,0:T(8,128)(2,1)S(1)}, bf16[16,64,512]{2,1,0:T(8,128)(2,1)S(1)}, bf16[16,64,512]{2,1,0:T(8,...) custom-call(s32[32]{0:T(128)} %order_hbm.1, ...), custom_call_target="tpu_custom_call" | custom-call | tf_op jit(solution)/shard_map/decoder/pallas_call | solution.py:770
  110.3 3.6 %finish.1 = (bf16[128,1024]{1,0:T(8,128)(2,1)}, f32[128,1024]{1,0:T(8,128)}, f32[8,128]{1,0:T(8,128)}, f32[8,128]{1,0:T(8,128)}, f32[3,1024,128]{2,1,0:T(8,128)}...) custom-call(bf16[128,1024]{1,0:T(8,128)(2,1)S(1)} %get-tuple-element, ...), custom_call_target="tpu_custom_call" | custom-call | tf_op jit(solution)/shard_map/finish/pallas_call | solution.py:890

commit v4 on v3

--- a/solution.py
+++ b/solution.py
@@ -23,10 +23,12 @@
     AGD,
     AGY,
     RKV,
-    RU,
+    RUX,
+    RUY,
     AGU,
     FWU,
-    RD,
+    RDY,
+    RDX,
     AGW,
     FWW,
     RB,
@@ -40,7 +42,7 @@
     AGG,
     AGV,
     NSEM,
-) = range(28)
+) = range(30)
 
 
 def nn(a, b):
@@ -134,11 +136,15 @@
     rkv,
     gu,
     pu,
-    ru,
+    rux,
+    tu,
+    ruy,
     ou,
     gd,
     pd,
-    rd,
+    rdy,
+    td,
+    rdx,
     od,
     gb,
     pb,
@@ -166,6 +172,9 @@
     core = lax.rem(ctx, 2)
     chip = lax.div(ctx, 2)
     other = 1 - core
+    row_at = lax.div(chip, 4)
+    col_at = lax.rem(chip, 4)
+    row_far = 1 - row_at
     slot = core * 8 + chip
     partner = chip * 2 + other
 
@@ -363,6 +372,164 @@
             lambda d: to_wa(buf.at[wa], buf.at[lax.rem(wa + 8 - d, 8)], kind, d).wait_recv(),
         )
 
+    def to_x(src, dst, kind, at, d):
+        return pltpu.make_async_remote_copy(
+            src_ref=src,
+            dst_ref=dst,
+            send_sem=ss.at[kind, at],
+            recv_sem=rs.at[kind, at],
+            device_id={"ctx": (row_at * 4 + lax.rem(col_at + d, 4)) * 2 + core},
+            device_id_type=MESH,
+        )
+
+    def to_y(src, dst, kind, at):
+        return pltpu.make_async_remote_copy(
+            src_ref=src,
+            dst_ref=dst,
+            send_sem=ss.at[kind, at],
+            recv_sem=rs.at[kind, at],
+            device_id={"ctx": lax.rem(chip + 4, 8) * 2 + core},
+            device_id_type=MESH,
+        )
+
+    def pair(buf, kept, index):
+        return pltpu.make_async_remote_copy(
+            src_ref=buf.at[other],
+            dst_ref=kept,
+            send_sem=cs_s.at[index],
+            recv_sem=cs_r.at[index],
+            device_id={"ctx": partner},
+            device_id_type=MESH,
+        )
+
+    def pair_start(buf, kept, index):
+        pair(buf, kept, index).start()
+        sends.append(lambda: pair(buf, kept, index).wait_send())
+        arrivals[100 + index] = lambda: pair_end(buf, kept, index)
+
+    def pair_end(buf, kept, index):
+        arrivals.pop(100 + index)
+        pair(buf, kept, index).wait_recv()
+
+        @pl.loop(0, 8)
+        def _(j):
+            at = (lax.div(j, 4), lax.rem(j, 4))
+            buf[(core, *at)] = (buf[(core, *at)].astype(F32) + kept[at].astype(F32)).astype(BF)
+
+    def up_x(d):
+        return to_x(gu.at[core, :, lax.rem(col_at + d, 4)], rux.at[d], RUX, d, d)
+
+    def up_start():
+        each(1, 4, lambda d: up_x(d).start())
+        sends.append(lambda: each(1, 4, lambda d: up_x(d).wait_send()))
+        arrivals[RUX] = up_mid
+
+    def up_mid():
+        arrivals.pop(RUX)
+        each(1, 4, lambda d: up_x(d).wait_recv())
+        for y in range(2):
+            whole = gu[core, y, col_at].astype(F32)
+            for d in range(1, 4):
+                whole = whole + rux[d, y].astype(F32)
+            tu[y] = whole.astype(BF)
+        to_y(tu.at[row_far], ruy, RUY, 0).start()
+        sends.append(lambda: to_y(tu.at[row_far], ruy, RUY, 0).wait_send())
+        arrivals[RUY] = up_end
+
+    def up_end():
+        arrivals.pop(RUY)
+        to_y(tu.at[row_far], ruy, RUY, 0).wait_recv()
+        ou[slot] = (tu[row_at].astype(F32) + ruy[...].astype(F32)).astype(BF)
+
+    def down_y():
+        return to_y(gd.at[core, row_far], rdy, RDY, 0)
+
+    def down_x(d):
+        return to_x(td.at[lax.rem(col_at + d, 4)], rdx.at[d], RDX, d, d)
+
+    def down_start():
+        down_y().start()
+        sends.append(lambda: down_y().wait_send())
+        arrivals[RDY] = down_mid
+
+    def down_mid():
+        arrivals.pop(RDY)
+        down_y().wait_recv()
+        for x in range(4):
+            td[x] = (gd[core, row_at, x].astype(F32) + rdy[x].astype(F32)).astype(BF)
+        each(1, 4, lambda d: down_x(d).start())
+        sends.append(lambda: each(1, 4, lambda d: down_x(d).wait_send()))
+        arrivals[RDX] = down_end
+
+    def down_end():
+        arrivals.pop(RDX)
+        each(1, 4, lambda d: down_x(d).wait_recv())
+        whole = td[col_at].astype(F32)
+        for d in range(1, 4):
+            whole = whole + rdx[d].astype(F32)
+        od[slot] = whole.astype(BF)
+
+    def place(side, y, d):
+        return side * 8 + y * 4 + lax.rem(col_at + 4 - d, 4)
+
+    def tree_start(buf, kind, forward, middle):
+        own = buf.at[slot]
+        to_y(own, own, kind, 4).start()
+        each(1, 4, lambda d: to_x(own, own, kind, d, d).start())
+        to_partner(own, own, kind, 0).start()
+
+        def sent():
+            each(0, 8, lambda d: to_y(own, own, kind, d).wait_send())
+            each(1, 8, lambda d: to_y(own, own, forward, d).wait_send())
+
+        sends.append(sent)
+        arrivals[kind] = lambda: (
+            middle(buf, kind, forward),
+            tree_pass(buf, kind, forward),
+            tree_end(buf, kind, forward),
+        )
+
+    def take(buf, s, kind, forward, d):
+        at = buf.at[s]
+        to_y(at, at, kind, d).wait_recv()
+        to_partner(at, at, forward, d).start()
+
+    def up_tree_mid(buf, kind, forward):
+        s = place(core, row_far, 0)
+        take(buf, s, kind, forward, 4)
+        each(1, 4, lambda d: to_x(buf.at[s], buf.at[s], kind, 4 + d, d).start())
+        each(1, 4, lambda d: take(buf, place(core, row_at, d), kind, forward, d))
+        arrivals[kind] = lambda: (tree_pass(buf, kind, forward), tree_end(buf, kind, forward))
+
+    def down_tree_mid(buf, kind, forward):
+        def step(d):
+            s = place(core, row_at, d)
+            take(buf, s, kind, forward, d)
+            to_y(buf.at[s], buf.at[s], kind, 4 + d).start()
+
+        each(1, 4, step)
+        take(buf, place(core, row_far, 0), kind, forward, 4)
+        arrivals[kind] = lambda: (tree_pass(buf, kind, forward), tree_end(buf, kind, forward))
+
+    def tree_pass(buf, kind, forward):
+        each(1, 4, lambda d: take(buf, place(core, row_far, d), kind, forward, 4 + d))
+        arrivals[kind] = lambda: tree_end(buf, kind, forward)
+
+    def tree_end(buf, kind, forward):
+        arrivals.pop(kind)
+
+        def landed(s, sem, d):
+            to_partner(buf.at[s], buf.at[s], sem, d).wait_recv()
+
+        landed(other * 8 + chip, kind, 0)
+        landed(place(other, row_far, 0), forward, 4)
+
+        def step(d):
+            landed(place(other, row_at, d), forward, d)
+            landed(place(other, row_far, d), forward, 4 + d)
+
+        each(1, 4, step)
+
     barrier = pltpu.get_barrier_semaphore()
     each(
         1,
@@ -513,12 +680,14 @@
     du = (dm[...] * slope).astype(BF)
     act = (0.5 * up * (1.0 + tanh)).astype(BF)
     reduce_start(nt(du, wup[...]), rs2s, rs2r, RS2)
-    gu[...] = tn(c_low, du).astype(BF).reshape(16, 64, 512)
-    combine_start(gu, pu, 0)
+    gu[...] = tn(c_low, du).astype(BF).reshape(2, 2, 4, 64, 512)
+    pair_start(gu, pu, 0)
     down = tn(act, g_ref[...]).astype(BF)
-    gd[:, 0:32, :] = down[:, 0:512].reshape(16, 32, 512)
-    gd[:, 32:64, :] = down[:, 512:1024].reshape(16, 32, 512)
-    combine_start(gd, pd, 1)
+    gd[:, :, :, 0:32, :] = down[:, 0:512].reshape(2, 2, 4, 32, 512)
+    gd[:, :, :, 32:64, :] = down[:, 512:1024].reshape(2, 2, 4, 32, 512)
+    pair_start(gd, pd, 1)
+    pair_end(gu, pu, 0)
+    up_start()
 
     def vec_row(r, value):
         for j in range(8):
@@ -535,15 +704,14 @@
     d_hidden = g_mine + norm_back(dc, ln2_gain, hat_two, rstd_two)
     dh_all[wa] = d_hidden.astype(BF)
     gather_start(dh_all, AGD)
-    combined(gu, pu, 0)
-    scatter_start(gu, ru, RU)
-    combined(gd, pd, 1)
-    scatter_start(gd, rd, RD)
+    pair_end(gd, pd, 1)
     vec_row(0, rows_sum(dc * hat_two))
     vec_row(1, rows_sum(dc))
     vec_row(2, rows_sum(d_hidden))
     vec_row(3, rows_sum(g_mine))
     gather_end(dh_all, AGD)
+    down_start()
+    up_mid()
 
     dh_low = dh_all[...].reshape(128, 1024)
     d_attn = nt(dh_low, wout[...]).astype(BF)
@@ -580,20 +748,25 @@
         gb[s, 0:64, :] = d_out[64 * (s % 2) : 64 * (s % 2) + 64, 128 * (s // 2) : 128 * (s // 2) + 128]
     combine_start(gb, pb, 3)
     reduce_start(nn(act, wdn[...]), rs3s, rs3r, RS3)
-    ou[slot] = scatter_end(gu, ru, RU)
-    od[slot] = scatter_end(gd, rd, RD)
+    combined(gb, pb, 3)
+    scatter_start(gb, rb, RB)
+    up_end()
+    tree_start(ou, AGU, FWU, up_tree_mid)
+    down_mid()
 
     dkv_mine = scatter_end(dkv, rkv, RKV)
-    d_qkv = jnp.concatenate([dq, dkv_mine], axis=1)
-    da = nt(d_qkv, wqkv[...])
-    reduce_start(da, rs4s, rs4r, RS4)
-    spread_start(ou, AGU, FWU)
     both = tn(normed[...], dkv_mine).astype(BF)
     gc[:, 0:64, :] = both[:, 0:128].reshape(16, 64, 128)
     gc[:, 64:128, :] = both[:, 128:256].reshape(16, 64, 128)
     combine_start(gc, pc, 4)
-    combined(gb, pb, 3)
-    scatter_start(gb, rb, RB)
+    d_qkv = jnp.concatenate([dq, dkv_mine], axis=1)
+    da = nt(d_qkv, wqkv[...])
+    reduce_start(da, rs4s, rs4r, RS4)
+    combined(gc, pc, 4)
+    scatter_start(gc, rc, RC)
+    down_end()
+    tree_start(od, AGW, FWW, down_tree_mid)
+    up_tree_mid(ou, AGU, FWU)
     vec_row(4, rows_sum(da * xhat_all[...]))
     vec_row(5, rows_sum(da))
     for j in range(8):
@@ -603,9 +776,8 @@
     cvs[12:13, :] = rows_sum(dq.astype(F32))
     cvs[13:14, :] = rows_sum(dkv_mine[:, 128:256].astype(F32))
     cvs[14:16, :] = jnp.zeros((2, 128), F32)
-    combined(gc, pc, 4)
-    scatter_start(gc, rc, RC)
-    spread_start(od, AGW, FWW)
+    ob[slot] = scatter_end(gb, rb, RB)
+    spread_start(ob, AGB, FWB)
 
     hat_one, rstd_one = normalize(x_mine)
     d_first = reduce_end(rs4s, rs4r, RS4)
@@ -631,11 +803,12 @@
 
     each(1, 16, lambda d: to_ctx(ctx, d).start())
     sends.append(lambda: each(1, 16, lambda d: to_ctx(ctx, d).wait_send()))
-    spread_pass(ou, AGU, FWU)
-    ob[slot] = scatter_end(gb, rb, RB)
-    spread_start(ob, AGB, FWB)
     oc[slot] = scatter_end(gc, rc, RC)
     spread_start(oc, AGCC, FWC)
+    down_tree_mid(od, AGW, FWW)
+    tree_pass(ou, AGU, FWU)
+    y_all[wa] = (hidden + reduce_end(rs3s, rs3r, RS3) + b_down).astype(BF)
+    gather_start(y_all, AGY)
     each(1, 16, lambda d: to_ctx(lax.rem(ctx + 16 - d, 16), d).wait_recv())
     ctx_sum = cvr[0]
     for i in range(1, 16):
@@ -643,26 +816,23 @@
     ctx_out[...] = ctx_sum[8:16, :]
     vall[wa] = ctx_sum[0:8, :]
     gather_start(vall, AGV)
-    spread_pass(od, AGW, FWW)
-    y_all[wa] = (hidden + reduce_end(rs3s, rs3r, RS3) + b_down).astype(BF)
-    gather_start(y_all, AGY)
     spread_pass(ob, AGB, FWB)
+    tree_end(ou, AGU, FWU)
+    ou_out[...] = ou[...]
+    tree_pass(od, AGW, FWW)
+    tree_end(od, AGW, FWW)
+    od_out[...] = od[...]
     spread_pass(oc, AGCC, FWC)
-
-    spread_end(ou, AGU, FWU)
-    ou_out[...] = ou[...]
-    spread_end(od, AGW, FWW)
-    od_out[...] = od[...]
-    gather_end(y_all, AGY)
-    y_out[...] = y_all[...].reshape(128, 1024)
     gather_end(g_all, AGG)
     gin_out[...] = g_all[...].reshape(128, 1024)
     spread_end(ob, AGB, FWB)
     ob_out[...] = ob[...]
+    gather_end(y_all, AGY)
+    y_out[...] = y_all[...].reshape(128, 1024)
+    gather_end(vall, AGV)
+    vec_out[...] = vall[...]
     spread_end(oc, AGCC, FWC)
     oc_out[...] = oc[...]
-    gather_end(vall, AGV)
-    vec_out[...] = vall[...]
 
     for sent in sends:
         sent()
@@ -821,13 +991,17 @@
             bf(16, 128, 256),
             bf(8, 128, 256),
             bf(8, 128, 256),
+            bf(2, 2, 4, 64, 512),
+            bf(2, 4, 64, 512),
+            bf(4, 2, 64, 512),
+            bf(2, 64, 512),
+            bf(64, 512),
             bf(16, 64, 512),
-            bf(8, 64, 512),
-            bf(8, 64, 512),
-            bf(16, 64, 512),
-            bf(16, 64, 512),
-            bf(8, 64, 512),
-            bf(8, 64, 512),
+            bf(2, 2, 4, 64, 512),
+            bf(2, 4, 64, 512),
+            bf(4, 64, 512),
+            bf(4, 64, 512),
+            bf(4, 64, 512),
             bf(16, 64, 512),
             bf(16, 128, 128),
             bf(8, 128, 128),

time: 114 us -> 101 us (0.89)
  Pallas kernels: 113 us -> 101 us
    pallas_call x1, Pallas kernels: 110 us -> 97 us  [body(): pl.pallas_call(layer, out_shape=(jax.ShapeDtypeStruct((128, 1024), BF), j...]
where the time goes in v4:
time: 101 us
  Pallas kernels  101 us (100%)
    pallas_call x1, Pallas kernels, body(): pl.pallas_call(layer, out_shape=(jax.ShapeDtypeStruct((128, 1024), BF), j...  97 us
    pallas_call x1, Pallas kernels, body(): pl.pallas_call(finish, out_shape=tuple((jax.ShapeDtypeStruct(*shape) for...  3.64 us

profile of v4, /device:TPU:1, one launch (start us, length us, event | category | flops | bytes accessed | tf_op | source)
XLA Modules:
  0.0 101.3 jit_solution(18001857031494872171)
XLA Ops:
  0.7 97.0 %decoder.1 = (bf16[128,1024]{1,0:T(8,128)(2,1)S(1)}, bf16[128,1024]{1,0:T(8,128)(2,1)S(1)}, bf16[16,64,512]{2,1,0:T(8,128)(2,1)S(1)}, bf16[16,64,512]{2,1,0:T(8,...) custom-call(s32[32]{0:T(128)} %order_hbm.1, ...), custom_call_target="tpu_custom_call" | custom-call | tf_op jit(solution)/shard_map/decoder/pallas_call | solution.py:940
  97.7 3.6 %finish.1 = (bf16[128,1024]{1,0:T(8,128)(2,1)}, f32[128,1024]{1,0:T(8,128)}, f32[8,128]{1,0:T(8,128)}, f32[8,128]{1,0:T(8,128)}, f32[3,1024,128]{2,1,0:T(8,128)}...) custom-call(bf16[128,1024]{1,0:T(8,128)(2,1)S(1)} %get-tuple-element, ...), custom_call_target="tpu_custom_call" | custom-call | tf_op jit(solution)/shard_map/finish/pallas_call | solution.py:1064

commit v5 on v4

--- a/solution.py
+++ b/solution.py
@@ -647,7 +647,7 @@
         acc[...] += tn(v_all[s], p.astype(BF))
         return total + jnp.sum(p.reshape(16, 8, 256), axis=0)
 
-    total = lax.fori_loop(0, 16, mix, jnp.zeros((8, 256), F32))
+    total = lax.fori_loop(0, 16, mix, jnp.zeros((8, 256), F32), unroll=16)
     total = jnp.sum(total, axis=0, keepdims=True)
     lse = top + jnp.log(total)
     half = lax.broadcasted_iota(jnp.int32, (128, 128), 0) < 64
@@ -735,11 +735,66 @@
         dkv[s, :, 0:128] = nn(ds, q2[...]).astype(BF)
         dkv[s, :, 128:256] = nn(p.astype(BF), do2).astype(BF)
 
-    each(0, 8, lambda j: back(other * 8 + j))
-    combine_start(dkv, pkv, 2)
-    each(0, 8, lambda j: back(core * 8 + j))
-    combined(dkv, pkv, 2)
-    scatter_start(dkv, rkv, RKV)
+    def send_half(side, y, index):
+        return pltpu.make_async_remote_copy(
+            src_ref=dkv.at[pl.ds(side * 8 + y * 4, 4)],
+            dst_ref=pkv.at[pl.ds(y * 4, 4)],
+            send_sem=cs_s.at[index],
+            recv_sem=cs_r.at[index],
+            device_id={"ctx": partner},
+            device_id_type=MESH,
+        )
+
+    def add_half(y, index):
+        send_half(other, y, index).wait_recv()
+
+        def step(j):
+            at = core * 8 + y * 4 + j
+            dkv[at] = (dkv[at].astype(F32) + pkv[y * 4 + j].astype(F32)).astype(BF)
+
+        each(0, 4, step)
+
+    def kv_near(d):
+        return to_x(dkv.at[core * 8 + row_at * 4 + lax.rem(col_at + d, 4)], rkv.at[d], RKV, d, d)
+
+    def kv_far(d):
+        return pltpu.make_async_remote_copy(
+            src_ref=dkv.at[core * 8 + row_far * 4 + lax.rem(col_at + d, 4)],
+            dst_ref=rkv.at[4 + d],
+            send_sem=ss.at[RKV, 4 + d],
+            recv_sem=rs.at[RKV, 4 + d],
+            device_id={"ctx": (row_far * 4 + lax.rem(col_at + d, 4)) * 2 + core},
+            device_id_type=MESH,
+        )
+
+    each(0, 4, lambda j: back(other * 8 + row_far * 4 + j))
+    send_half(other, row_far, 2).start()
+    each(0, 4, lambda j: back(core * 8 + row_far * 4 + j))
+    each(0, 4, lambda j: back(other * 8 + row_at * 4 + j))
+    send_half(other, row_at, 21).start()
+    add_half(row_far, 2)
+    each(0, 4, lambda d: kv_far(d).start())
+    up_end()
+    tree_start(ou, AGU, FWU, up_tree_mid)
+    each(0, 4, lambda j: back(core * 8 + row_at * 4 + j))
+    add_half(row_at, 21)
+    each(1, 4, lambda d: kv_near(d).start())
+
+    def kv_sent():
+        send_half(other, row_far, 2).wait_send()
+        send_half(other, row_at, 21).wait_send()
+        each(0, 4, lambda d: kv_far(d).wait_send())
+        each(1, 4, lambda d: kv_near(d).wait_send())
+
+    sends.append(kv_sent)
+
+    def kv_end():
+        each(1, 4, lambda d: kv_near(d).wait_recv())
+        each(0, 4, lambda d: kv_far(d).wait_recv())
+        whole = dkv[slot].astype(F32)
+        for d in range(1, 8):
+            whole = whole + rkv[d].astype(F32)
+        return whole.astype(BF)
 
     dq = (diagonal(acc[...]) * 0.125).T.astype(BF)
     gb[:, 64:128, :] = tn(normed[...], dq).astype(BF).reshape(16, 64, 128)
@@ -750,11 +805,9 @@
     reduce_start(nn(act, wdn[...]), rs3s, rs3r, RS3)
     combined(gb, pb, 3)
     scatter_start(gb, rb, RB)
-    up_end()
-    tree_start(ou, AGU, FWU, up_tree_mid)
     down_mid()
 
-    dkv_mine = scatter_end(dkv, rkv, RKV)
+    dkv_mine = kv_end()
     both = tn(normed[...], dkv_mine).astype(BF)
     gc[:, 0:64, :] = both[:, 0:128].reshape(16, 64, 128)
     gc[:, 64:128, :] = both[:, 128:256].reshape(16, 64, 128)
@@ -818,10 +871,11 @@
     gather_start(vall, AGV)
     spread_pass(ob, AGB, FWB)
     tree_end(ou, AGU, FWU)
-    ou_out[...] = ou[...]
+    ou_out[...] = ou[...].astype(F32).reshape(1024, 512)
     tree_pass(od, AGW, FWW)
     tree_end(od, AGW, FWW)
-    od_out[...] = od[...]
+    od_out[:, 0:512] = od[:, 0:32, :].astype(F32).reshape(512, 512)
+    od_out[:, 512:1024] = od[:, 32:64, :].astype(F32).reshape(512, 512)
     spread_pass(oc, AGCC, FWC)
     gather_end(g_all, AGG)
     gin_out[...] = g_all[...].reshape(128, 1024)
@@ -864,8 +918,6 @@
     gin,
     gqkv,
     gwo,
-    gup,
-    gdn,
     sems,
 ):
     copies = []
@@ -875,16 +927,8 @@
         copies[-1].start()
 
     leave(y_ref, y_out)
-    for i in range(4):
-        rows = pl.ds(256 * i, 256)
-        gup[rows, :] = ou_ref[4 * i : 4 * i + 4].astype(F32).reshape(256, 512)
-        leave(gup.at[rows], gup_out.at[rows])
-    for i in range(4):
-        rows = pl.ds(128 * i, 128)
-        part = od_ref[4 * i : 4 * i + 4].astype(F32)
-        gdn[rows, 0:512] = part[:, 0:32].reshape(128, 512)
-        gdn[rows, 512:1024] = part[:, 32:64].reshape(128, 512)
-        leave(gdn.at[rows], gdn_out.at[rows])
+    leave(ou_ref, gup_out)
+    leave(od_ref, gdn_out)
     gin[...] = gin_ref[...].astype(F32)
     leave(gin, gin_out)
     for s in range(16):
@@ -942,8 +986,8 @@
         out_shape=(
             jax.ShapeDtypeStruct((128, 1024), BF),
             jax.ShapeDtypeStruct((128, 1024), BF),
-            jax.ShapeDtypeStruct((16, 64, 512), BF),
-            jax.ShapeDtypeStruct((16, 64, 512), BF),
+            jax.ShapeDtypeStruct((1024, 512), F32),
+            jax.ShapeDtypeStruct((512, 1024), F32),
             jax.ShapeDtypeStruct((16, 128, 128), BF),
             jax.ShapeDtypeStruct((16, 128, 128), BF),
             jax.ShapeDtypeStruct((8, 8, 128), F32),
@@ -1021,8 +1065,8 @@
             f32(16, 16, 128),
             pltpu.SemaphoreType.DMA((NSEM, 8)),
             pltpu.SemaphoreType.DMA((NSEM, 8)),
-            pltpu.SemaphoreType.DMA((21,)),
-            pltpu.SemaphoreType.DMA((21,)),
+            pltpu.SemaphoreType.DMA((22,)),
+            pltpu.SemaphoreType.DMA((22,)),
         ],
         compiler_params=pltpu.CompilerParams(
             collective_id=0, has_side_effects=True, vmem_limit_bytes=32 << 20
@@ -1070,8 +1114,6 @@
                 f32(128, 1024),
                 f32(3, 1024, 128),
                 f32(128, 1024),
-                f32(1024, 512),
-                f32(512, 1024),
                 pltpu.SemaphoreType.DMA((14,)),
             ],
             compiler_params=pltpu.CompilerParams(vmem_limit_bytes=24 << 20),

time: 101 us -> 96.8 us (0.958)
  Pallas kernels: 101 us -> 96 us
    pallas_call x1, Pallas kernels: 97 us -> 92.4 us  [body(): pl.pallas_call(layer, out_shape=(jax.ShapeDtypeStruct((128, 1024), BF), j...]
where the time goes in v5:
time: 96.8 us; the launch traced here: 96.7 us
  Pallas kernels  96 us (99%)
    pallas_call x1, Pallas kernels, body(): pl.pallas_call(layer, out_shape=(jax.ShapeDtypeStruct((128, 1024), BF), j...  92.4 us
    pallas_call x1, Pallas kernels, body(): pl.pallas_call(finish, out_shape=tuple((jax.ShapeDtypeStruct(*shape) for...  3.65 us

profile of v5, /device:TPU:1, one launch (start us, length us, event | category | flops | bytes accessed | tf_op | source)
XLA Modules:
  0.0 96.7 jit_solution(8738155563992030723)
XLA Ops:
  0.7 92.4 %decoder.1 = (bf16[128,1024]{1,0:T(8,128)(2,1)S(1)}, bf16[128,1024]{1,0:T(8,128)(2,1)S(1)}, f32[1024,512]{1,0:T(8,128)S(1)}, f32[512,1024]{1,0:T(8,128)S(1)}, bf...) custom-call(s32[32]{0:T(128)} %order_hbm.1, ...), custom_call_target="tpu_custom_call" | custom-call | tf_op jit(solution)/shard_map/decoder/pallas_call | solution.py:984
  93.1 3.6 %finish.1 = (bf16[128,1024]{1,0:T(8,128)(2,1)}, f32[128,1024]{1,0:T(8,128)}, f32[8,128]{1,0:T(8,128)}, f32[8,128]{1,0:T(8,128)}, f32[3,1024,128]{2,1,0:T(8,128)}...) custom-call(bf16[128,1024]{1,0:T(8,128)(2,1)S(1)} %get-tuple-element, ...), custom_call_target="tpu_custom_call" | custom-call | tf_op jit(solution)/shard_map/finish/pallas_call | solution.py:1108

commit v6 on v5

--- a/solution.py
+++ b/solution.py
@@ -30,6 +30,7 @@
     RDY,
     RDX,
     AGW,
+    AGX,
     FWW,
     RB,
     AGB,
@@ -42,7 +43,7 @@
     AGG,
     AGV,
     NSEM,
-) = range(30)
+) = range(31)
 
 
 def nn(a, b):
@@ -472,7 +473,7 @@
     def place(side, y, d):
         return side * 8 + y * 4 + lax.rem(col_at + 4 - d, 4)
 
-    def tree_start(buf, kind, forward, middle):
+    def tree_start(buf, kind, forward, middle, sent_all=None):
         own = buf.at[slot]
         to_y(own, own, kind, 4).start()
         each(1, 4, lambda d: to_x(own, own, kind, d, d).start())
@@ -482,7 +483,7 @@
             each(0, 8, lambda d: to_y(own, own, kind, d).wait_send())
             each(1, 8, lambda d: to_y(own, own, forward, d).wait_send())
 
-        sends.append(sent)
+        sends.append(sent if sent_all is None else lambda: sent_all(buf, kind, forward))
         arrivals[kind] = lambda: (
             middle(buf, kind, forward),
             tree_pass(buf, kind, forward),
@@ -505,11 +506,35 @@
         def step(d):
             s = place(core, row_at, d)
             take(buf, s, kind, forward, d)
-            to_y(buf.at[s], buf.at[s], kind, 4 + d).start()
+            top = buf.at[s, pl.ds(0, 32)]
+            to_y(top, top, kind, 4 + d).start()
 
         each(1, 4, step)
-        take(buf, place(core, row_far, 0), kind, forward, 4)
-        arrivals[kind] = lambda: (tree_pass(buf, kind, forward), tree_end(buf, kind, forward))
+        s = place(core, row_far, 0)
+        take(buf, s, kind, forward, 4)
+        low = buf.at[s, pl.ds(32, 32)]
+        each(1, 4, lambda d: to_x(low, low, AGX, d, d).start())
+        arrivals[kind] = lambda: (down_tree_pass(buf, kind, forward), tree_end(buf, kind, forward))
+
+    def down_tree_pass(buf, kind, forward):
+        def step(d):
+            s = place(core, row_far, d)
+            top = buf.at[s, pl.ds(0, 32)]
+            low = buf.at[s, pl.ds(32, 32)]
+            to_y(top, top, kind, 4 + d).wait_recv()
+            to_y(low, low, AGX, d).wait_recv()
+            to_partner(buf.at[s], buf.at[s], forward, 4 + d).start()
+
+        each(1, 4, step)
+        arrivals[kind] = lambda: tree_end(buf, kind, forward)
+
+    def down_tree_sent(buf, kind, forward):
+        own = buf.at[slot]
+        part = buf.at[slot, pl.ds(0, 32)]
+        each(0, 5, lambda d: to_y(own, own, kind, d).wait_send())
+        each(1, 8, lambda d: to_y(own, own, forward, d).wait_send())
+        each(5, 8, lambda d: to_y(part, part, kind, d).wait_send())
+        each(1, 4, lambda d: to_y(part, part, AGX, d).wait_send())
 
     def tree_pass(buf, kind, forward):
         each(1, 4, lambda d: take(buf, place(core, row_far, d), kind, forward, 4 + d))
@@ -808,17 +833,17 @@
     down_mid()
 
     dkv_mine = kv_end()
+    d_qkv = jnp.concatenate([dq, dkv_mine], axis=1)
+    da = nt(d_qkv, wqkv[...])
+    reduce_start(da, rs4s, rs4r, RS4)
     both = tn(normed[...], dkv_mine).astype(BF)
     gc[:, 0:64, :] = both[:, 0:128].reshape(16, 64, 128)
     gc[:, 64:128, :] = both[:, 128:256].reshape(16, 64, 128)
     combine_start(gc, pc, 4)
-    d_qkv = jnp.concatenate([dq, dkv_mine], axis=1)
-    da = nt(d_qkv, wqkv[...])
-    reduce_start(da, rs4s, rs4r, RS4)
     combined(gc, pc, 4)
     scatter_start(gc, rc, RC)
     down_end()
-    tree_start(od, AGW, FWW, down_tree_mid)
+    tree_start(od, AGW, FWW, down_tree_mid, down_tree_sent)
     up_tree_mid(ou, AGU, FWU)
     vec_row(4, rows_sum(da * xhat_all[...]))
     vec_row(5, rows_sum(da))
@@ -872,11 +897,11 @@
     spread_pass(ob, AGB, FWB)
     tree_end(ou, AGU, FWU)
     ou_out[...] = ou[...].astype(F32).reshape(1024, 512)
-    tree_pass(od, AGW, FWW)
+    spread_pass(oc, AGCC, FWC)
+    down_tree_pass(od, AGW, FWW)
     tree_end(od, AGW, FWW)
     od_out[:, 0:512] = od[:, 0:32, :].astype(F32).reshape(512, 512)
     od_out[:, 512:1024] = od[:, 32:64, :].astype(F32).reshape(512, 512)
-    spread_pass(oc, AGCC, FWC)
     gather_end(g_all, AGG)
     gin_out[...] = g_all[...].reshape(128, 1024)
     spread_end(ob, AGB, FWB)

time: 96.8 us -> 96.1 us (level)
  no operation moved by 1% of the time
where the time goes in v6:
time: 96.1 us; the launch traced here: 96 us
  Pallas kernels  95.3 us (99%)
    pallas_call x1, Pallas kernels, body(): pl.pallas_call(layer, out_shape=(jax.ShapeDtypeStruct((128, 1024), BF), j...  91.7 us
    pallas_call x1, Pallas kernels, body(): pl.pallas_call(finish, out_shape=tuple((jax.ShapeDtypeStruct(*shape) for...  3.65 us

profile of v6, /device:TPU:1, one launch (start us, length us, event | category | flops | bytes accessed | tf_op | source)
XLA Modules:
  0.0 96.0 jit_solution(15465494197943925684)
XLA Ops:
  0.7 91.7 %decoder.1 = (bf16[128,1024]{1,0:T(8,128)(2,1)S(1)}, bf16[128,1024]{1,0:T(8,128)(2,1)S(1)}, f32[1024,512]{1,0:T(8,128)S(1)}, f32[512,1024]{1,0:T(8,128)S(1)}, bf...) custom-call(s32[32]{0:T(128)} %order_hbm.1, ...), custom_call_target="tpu_custom_call" | custom-call | tf_op jit(solution)/shard_map/decoder/pallas_call | solution.py:1009
  92.3 3.6 %finish.1 = (bf16[128,1024]{1,0:T(8,128)(2,1)}, f32[128,1024]{1,0:T(8,128)}, f32[8,128]{1,0:T(8,128)}, f32[8,128]{1,0:T(8,128)}, f32[3,1024,128]{2,1,0:T(8,128)}...) custom-call(bf16[128,1024]{1,0:T(8,128)(2,1)S(1)} %get-tuple-element, ...), custom_call_target="tpu_custom_call" | custom-call | tf_op jit(solution)/shard_map/finish/pallas_call | solution.py:1133
